TPU v7x, 32 devices: a whole 2x2x4 slice. The times are simulated.
32 devices in a mesh: groups: 2 (over y), dp: 8 (over z, x), section: 2 (over core).
Axes of the slice: x: 2, y: 2, z: 4, core: 2. Of those that a mesh axis runs over, the one named last changes fastest.
Arguments:
- latents: bfloat16 [2048, 3072], P(('groups', 'dp')), parts along dimension 0, may hold values from -6 to 6
- out_grad: float32 [2048, 3072], P(('groups', 'dp')), parts along dimension 0, may hold values from -0.3 to 0.3
- frozen_weight: bfloat16 [2, 3072, 1536], P('section', 'dp'), may hold values from -0.109375 to 0.109375
- norm_gain: float32 [2, 3072], P('section'), may hold values from 0.5 to 1.5
- time_gate: float32 [2, 50], P('section'), may hold values from 0.5 to 2
- down_factors: bfloat16 [2, 96, 64, 3072], P('section', ('groups', 'dp')), parts along dimension 1, may hold values from -0.109375 to 0.109375
- up_factors: bfloat16 [2, 96, 64, 1536], P('section', ('groups', 'dp')), parts along dimension 1, may hold values from -0.75 to 0.75
- block_jobs: int32 [16], P('groups'), parts along dimension 0, may hold values from 0 to 47
- owners: int32 [96], P('groups'), parts along dimension 0, may hold values from 0 to 47, as said below
- block_steps: int32 [16], P(('groups', 'dp')), parts along dimension 0, may hold values from 0 to 49
- block_fill: int32 [16], P(('groups', 'dp')), parts along dimension 0, may hold values from 1 to 128, as said below
Outputs:
- grad_down: float32 [2, 96, 64, 3072], P('section', ('groups', 'dp')), parts along dimension 1
- grad_up: float32 [2, 96, 64, 1536], P('section', ('groups', 'dp')), parts along dimension 1
There are 2 independent parts, one for each index of `groups`. A program takes and returns all parts, laid end to end along the dimension named above; an argument that names none is the same for every part. Nothing has to cross between parts.
Inputs may be any that keep to these rules, and one draw needn't show every extreme that they name: `owners`: no two adapters share a slot; slot 0 and the last slot always hold one. `block_fill`: the live rows come first in their block; in every draw some block is full and some holds a single live row.
All inputs are finite; a program needn't handle non-finite values.
Results may differ from a plain program's by a relative error of at most 0.006.
Values may be sent and summed in bfloat16 or wider, within the bound.
No kernel may reach another device: no remote copies, remote signals or barrier semaphores. Data moves between devices by JAX's collectives and lax.ppermute only.
A program may use at most 128 MiB of HBM per device.

v0:
```python
import jax
import jax.numpy as jnp
from jax import lax
from jax.sharding import PartitionSpec as P

epsilon = 1e-06


def passed_along(value, axis, steps):
    count = lax.axis_size(axis)
    leading, last = (max(0, -steps), min(count, count - steps))
    return lax.ppermute(value, axis, [(source, source + steps) for source in range(leading, last)])


def matrix_product(spec, left_op, right_op):
    return jnp.einsum(spec, left_op, right_op, preferred_element_type=jnp.float32)


def forward_pass(inputs, frozen_layer, gain_row, down_projection_block, up_block, scales):
    out_width = up_block.shape[2]
    block_total, row_count, model_width = inputs.shape
    values = inputs.astype(jnp.float32)
    inverse = lax.rsqrt(jnp.mean(values * values, axis=2) + epsilon)
    normalized_input = (values * inverse[:, :, None] * gain_row).astype(jnp.bfloat16)
    frozen_out = jnp.dot(
        normalized_input.reshape(block_total * row_count, model_width),
        frozen_layer,
        preferred_element_type=jnp.float32,
    )
    frozen_out = frozen_out.reshape(block_total, row_count, out_width)
    reduced_features = matrix_product(
        "uyi,uoi->uyo", normalized_input, down_projection_block
    ).astype(jnp.bfloat16)
    extra = matrix_product("bmq,bqh->bmh", reduced_features, up_block)
    update = scales[:, None, None] * (frozen_out + extra)
    window_out = (values[:, :, :out_width] + update).astype(jnp.bfloat16)
    outputs = jnp.concatenate([window_out, inputs[:, :, out_width:]], axis=2)
    return (outputs, (inputs, normalized_input, inverse, reduced_features))


def backward_pass(
    stored, cotangent, frozen_layer, gain_row, down_projection_block, up_block, scales
):
    inputs, normalized_input, inverse, reduced_features = stored
    out_width = up_block.shape[2]
    block_total, row_count, model_width = inputs.shape
    values = inputs.astype(jnp.float32)
    delta_output = (scales[:, None, None] * cotangent[:, :, :out_width]).astype(jnp.bfloat16)
    grad_upper = matrix_product("bmq,bmh->bqh", reduced_features, delta_output)
    low_rank_delta = matrix_product("bmh,bqh->bmq", delta_output, up_block).astype(jnp.bfloat16)
    lower_gradient = matrix_product("hoc,hou->hcu", low_rank_delta, normalized_input)
    through = lax.dot_general(
        delta_output.reshape(block_total * row_count, out_width),
        frozen_layer,
        (((1,), (1,)), ((), ())),
        preferred_element_type=jnp.float32,
    )
    delta_normalized = through.reshape(block_total, row_count, model_width) + matrix_product(
        "rha,rak->rhk", low_rank_delta, down_projection_block
    )
    scaled = gain_row * delta_normalized
    inner = jnp.mean(values * scaled, axis=2)
    cubed = inverse * inverse * inverse
    delta_in = inverse[:, :, None] * scaled - values * (cubed * inner)[:, :, None]
    carried = (cotangent + delta_in).astype(jnp.bfloat16)
    return (carried, lower_gradient, grad_upper)


def body(
    latents,
    out_grad,
    frozen_weight,
    norm_gain,
    time_gate,
    down_factors,
    up_factors,
    block_jobs,
    owners,
    block_steps,
    block_fill,
):
    position = lax.axis_index("section")
    lane_count = lax.axis_size("dp")
    slot_local = down_factors.shape[1]
    low_rank = down_factors.shape[2]
    model_width = down_factors.shape[3]
    blocks_dev = block_fill.shape[0]
    block_rows = latents.shape[0] // blocks_dev
    is_first = position == 0
    frozen_layer = lax.all_gather(frozen_weight[0], "dp", axis=0, tiled=True)
    gain_row = norm_gain[0]
    gate_row = time_gate[0]
    chosen = block_steps[:, None] == jnp.arange(gate_row.shape[0], dtype=jnp.int32)[None, :]
    scales = jnp.sum(jnp.where(chosen, gate_row[None, :], 0.0), axis=1)
    matches = block_jobs[:, None] == jnp.arange(owners.shape[0], dtype=jnp.int32)[None, :]
    slot_of = jnp.sum(jnp.where(matches, owners[None, :], 0), axis=1)
    spread_down, spread_up = (
        lax.all_to_all(down_factors[0], "dp", split_axis=2, concat_axis=0, tiled=True),
        lax.all_to_all(up_factors[0], "dp", split_axis=2, concat_axis=0, tiled=True),
    )
    down_projection_block, up_block = (
        lax.all_to_all(spread_down[slot_of], "dp", split_axis=0, concat_axis=2, tiled=True),
        lax.all_to_all(spread_up[slot_of], "dp", split_axis=0, concat_axis=2, tiled=True),
    )
    micro_count = 1
    micro_rows = block_rows // micro_count
    block_view = latents.reshape(blocks_dev, block_rows, model_width)
    live_rows = jnp.arange(block_rows, dtype=jnp.int32)[None, :] < block_fill[:, None]
    masked = jnp.where(
        live_rows[:, :, None], out_grad.reshape(blocks_dev, block_rows, model_width), 0.0
    )
    incoming = jnp.zeros((blocks_dev, micro_rows, model_width), jnp.bfloat16)
    kept = []
    for turn_index in range(micro_count + 1):
        source = jnp.where(is_first, block_view, incoming)
        outputs, stored = forward_pass(
            source, frozen_layer, gain_row, down_projection_block, up_block, scales
        )
        kept.append(stored)
        if turn_index < micro_count:
            incoming = passed_along(outputs, "section", 1)
    states = [
        jax.tree.map(lambda former, latter: jnp.where(is_first, former, latter), kept[0], kept[1])
    ]
    returned = jnp.zeros((blocks_dev, micro_rows, model_width), jnp.bfloat16)
    sum_down = jnp.zeros((blocks_dev, low_rank, model_width), jnp.float32)
    sum_up = jnp.zeros((blocks_dev, low_rank, up_block.shape[2]), jnp.float32)
    for turn_index in range(micro_count + 1):
        late_micro = min(turn_index, micro_count - 1)
        early_micro = max(turn_index - 1, 0)
        current = jax.tree.map(
            lambda former, latter: jnp.where(is_first, former, latter),
            states[early_micro],
            states[late_micro],
        )
        cotangent = jnp.where(is_first, returned.astype(jnp.float32), masked)
        carried, lower_gradient, grad_upper = backward_pass(
            current, cotangent, frozen_layer, gain_row, down_projection_block, up_block, scales
        )
        useful = jnp.where(is_first, turn_index >= 1, turn_index < micro_count)
        sum_down = sum_down + jnp.where(useful, lower_gradient, 0.0)
        sum_up = sum_up + jnp.where(useful, grad_upper, 0.0)
        if turn_index < micro_count:
            returned = passed_along(carried, "section", -1)
    pieces_down, pieces_up = (
        lax.all_to_all(sum_down, "dp", split_axis=2, concat_axis=0, tiled=True),
        lax.all_to_all(sum_up, "dp", split_axis=2, concat_axis=0, tiled=True),
    )
    slot_total = lane_count * slot_local
    onehot = (jnp.arange(slot_total, dtype=jnp.int32)[:, None] == slot_of[None, :]).astype(
        jnp.float32
    )
    block_total = pieces_down.shape[0]
    slot_down = jnp.dot(
        onehot,
        pieces_down.reshape(block_total, -1),
        precision=lax.Precision.HIGHEST,
        preferred_element_type=jnp.float32,
    )
    slot_up = jnp.dot(
        onehot,
        pieces_up.reshape(block_total, -1),
        precision=lax.Precision.HIGHEST,
        preferred_element_type=jnp.float32,
    )
    slot_down = slot_down.reshape(slot_total, low_rank, pieces_down.shape[2])
    slot_up = slot_up.reshape(slot_total, low_rank, pieces_up.shape[2])
    owned_down, owned_up = (
        lax.all_to_all(slot_down, "dp", split_axis=0, concat_axis=2, tiled=True),
        lax.all_to_all(slot_up, "dp", split_axis=0, concat_axis=2, tiled=True),
    )
    return (owned_down[None], owned_up[None])


def solution(mesh):
    placed = (
        P(("groups", "dp"), None),
        P(("groups", "dp"), None),
        P("section", "dp", None),
        P("section", None),
        P("section", None),
        P("section", ("groups", "dp"), None, None),
        P("section", ("groups", "dp"), None, None),
        P("groups"),
        P("groups"),
        P(("groups", "dp")),
        P(("groups", "dp")),
    )
    return jax.shard_map(
        body,
        mesh=mesh,
        in_specs=placed,
        out_specs=(
            P("section", ("groups", "dp"), None, None),
            P("section", ("groups", "dp"), None, None),
        ),
        check_vma=False,
    )
```

profile of v0, /device:TPU:0, one launch (start us, length us, event | category | flops | bytes accessed | tf_op | source)
XLA Modules:
  0.0 537.3 jit_solution(2931471331591064361)
XLA Ops:
  8.4 3.4 copy.64
  11.9 2.0 bitcast_bitcast_fusion.1
  13.9 3.1 reshape.236
  17.0 7.5 %all-to-all-start = ((bf16[8,2,36864]{2,1,0:T(2,128)(2,1)}), bf16[8,2,36864]{2,1,0:T(2,128)(2,1)S(1)}, u32[]{:S(2)}, u32[]{:S(2)}) async-start(bf16[8,2,36864]{2,1,0:T(2,128)(2,1)} %reshape.236), calls=%async_computation | async-start | bytes 2359296 | tf_op jit(solution)/shard_map/all_to_all | solution.py:99
  24.5 6.0 %copy.68 = bf16[1,6,64,3072]{2,1,3,0:T(8,128)(2,1)} copy(bf16[1,6,64,3072]{3,2,1,0:T(8,128)(2,1)S(1)} %copy-done.7) | data formatting | bytes 4718592 | tf_op args[5]
  30.5 6.4 %bitcast_bitcast_fusion = bf16[3072,6,64]{2,1,0:T(8,128)(2,1)} fusion(bf16[1,6,64,3072]{2,1,3,0:T(8,128)(2,1)} %copy.68), kind=kLoop, calls=%fused_computation.81 | loop fusion | bytes 4718592
  37.0 8.5 %reshape.238 = bf16[8,2,73728]{2,1,0:T(2,128)(2,1)} reshape(bf16[3072,6,64]{2,1,0:T(8,128)(2,1)} %bitcast_bitcast_fusion) | data formatting | bytes 4718592
  45.5 38.7 %all-to-all-done = bf16[8,2,36864]{2,1,0:T(2,128)(2,1)S(1)} async-done(((bf16[8,2,36864]{2,1,0:T(2,128)(2,1)}), bf16[8,2,36864]{2,1,0:T(2,128)(2,1)S(1)}, u32[]{:S(2)}, u32[]{:S(2)}) %all-to-all-start) | async-done | bytes 1179680 | tf_op jit(solution)/shard_map/all_to_all | solution.py:99
  85.2 4.4 all-to-all-start.2
  91.0 2.1 select_bitcast_fusion
  93.1 3.6 reshape.237
  96.6 2.7 copy.66
  99.3 2.7 gather_fusion
  102.1 98.8 %all-to-all-done.2 = bf16[8,2,73728]{2,1,0:T(2,128)(2,1)} async-done(((bf16[8,2,73728]{2,1,0:T(2,128)(2,1)}), bf16[8,2,73728]{2,1,0:T(2,128)(2,1)}, u32[]{:S(2)}, u32[]{:S(2)}) %all-to-all-start.2) | async-done | bytes 2359328 | tf_op jit(solution)/shard_map/all_to_all | solution.py:98
  200.9 9.0 %all-to-all-start.1 = ((bf16[8,64,192]{2,1,0:T(8,128)(2,1)}), bf16[8,64,192]{2,1,0:T(8,128)(2,1)S(1)}, u32[]{:S(2)}, u32[]{:S(2)}) async-start(bf16[8,64,192]{2,1,0:T(8,128)(2,1)} %gather_fusion), calls=%async_computation.1 | async-start | bytes 524288 | tf_op jit(solution)/shard_map/all_to_all | solution.py:103
  213.6 8.2 %reshape.239 = bf16[3072,6,64]{2,1,0:T(8,128)(2,1)} reshape(bf16[8,2,73728]{2,1,0:T(2,128)(2,1)} %all-to-all-done.2) | data formatting | bytes 4718592
  221.9 6.7 %copy.70 = bf16[8,6,64,384]{3,2,1,0:T(8,128)(2,1)} copy(bf16[8,6,64,384]{2,1,3,0:T(8,128)(2,1)} %bitcast.151) | data formatting | bytes 4718592 | tf_op jit(solution)/shard_map/all_to_all | solution.py:98
  228.5 3.1 gather_fusion.1
  231.7 6.0 %all-to-all-start.3 = ((bf16[8,64,384]{2,1,0:T(8,128)(2,1)}), bf16[8,64,384]{2,1,0:T(8,128)(2,1)S(1)}, u32[]{:S(2)}, u32[]{:S(2)}) async-start(bf16[8,64,384]{2,1,0:T(8,128)(2,1)} %gather_fusion.1), calls=%async_computation.3 | async-start | bytes 786432 | tf_op jit(solution)/shard_map/all_to_all | solution.py:102
  238.3 1.8 copy.67
  241.3 7.4 %all-to-all-done.3 = bf16[8,64,384]{2,1,0:T(8,128)(2,1)S(1)} async-done(((bf16[8,64,384]{2,1,0:T(8,128)(2,1)}), bf16[8,64,384]{2,1,0:T(8,128)(2,1)S(1)}, u32[]{:S(2)}, u32[]{:S(2)}) %all-to-all-start.3) | async-done | bytes 393248 | tf_op jit(solution)/shard_map/all_to_all | solution.py:102
  250.1 5.3 fusion.2
  258.7 3.1 fusion
  269.3 1.6 fusion.34
  272.9 7.1 %reduce.7 = f32[1536,64]{1,0:T(8,128)S(1)} reduce(f32[1536,1,64]{2,1,0:T(1,128)S(1)} %bitcast.157, f32[]{:T(128)} %broadcast.202), dimensions={1}, to_apply=%bitcast.124.reduce_sub_computation | reduce | bytes 786436
  281.3 4.1 all-to-all-start.6
  285.4 1.7 convolution_select_fusion
  287.1 1.8 fusion.6
  288.9 1.7 copy.72
  290.6 13.6 %reduce.5 = f32[3072,64]{1,0:T(8,128)S(1)} reduce(f32[3072,1,64]{2,1,0:T(1,128)S(1)} %bitcast.155, f32[]{:T(128)} %broadcast.202), dimensions={1}, to_apply=%bitcast.122.reduce_sub_computation | reduce | bytes 1572868
  304.2 1.9 reshape.240
  306.0 6.1 %all-to-all-start.4 = ((f32[8,1,24576]{2,1,0:T(1,128)}), f32[8,1,24576]{2,1,0:T(1,128)S(1)}, u32[]{:S(2)}, u32[]{:S(2)}) async-start(f32[8,1,24576]{2,1,0:T(1,128)} %reshape.240), calls=%async_computation.4 | async-start | bytes 1572864 | tf_op jit(solution)/shard_map/all_to_all | solution.py:146
  312.2 2.5 reduce.8
  318.0 3.5 copy.79
  321.5 11.2 %all-to-all-done.4 = f32[8,1,24576]{2,1,0:T(1,128)S(1)} async-done(((f32[8,1,24576]{2,1,0:T(1,128)}), f32[8,1,24576]{2,1,0:T(1,128)S(1)}, u32[]{:S(2)}, u32[]{:S(2)}) %all-to-all-start.4) | async-done | bytes 786464 | tf_op jit(solution)/shard_map/all_to_all | solution.py:146
  333.5 3.9 all-to-all-start.7
  337.5 4.4 reduce.6
  341.9 4.2 reshape.241
  346.2 2.7 copy.73
  348.9 3.3 fusion.37
  352.2 3.6 copy.74
  355.8 52.5 %all-to-all-done.7 = f32[48,64,192]{2,1,0:T(8,128)S(1)} async-done(((f32[48,64,192]{2,1,0:T(8,128)}), f32[48,64,192]{2,1,0:T(8,128)S(1)}, u32[]{:S(2)}, u32[]{:S(2)}) %all-to-all-start.7) | async-done | bytes 2359328 | tf_op jit(solution)/shard_map/all_to_all | solution.py:170
  408.3 4.9 all-to-all-start.5
  413.2 3.5 copy.80
  416.7 4.3 broadcast_in_dim.68
  421.0 96.0 %all-to-all-done.5 = f32[48,64,384]{2,1,0:T(8,128)} async-done(((f32[48,64,384]{2,1,0:T(8,128)}), f32[48,64,384]{2,1,0:T(8,128)}, u32[]{:S(2)}, u32[]{:S(2)}) %all-to-all-start.5) | async-done | bytes 4718624 | tf_op jit(solution)/shard_map/all_to_all | solution.py:169
  517.0 7.2 %copy.75 = f32[6,64,8,384]{3,2,1,0:T(8,128)} copy(f32[6,64,8,384]{3,1,0,2:T(8,128)} %bitcast.39) | data formatting | bytes 9437184 | tf_op jit(solution)/shard_map/all_to_all | solution.py:169
  524.2 5.8 %broadcast_in_dim.66 = f32[1,6,64,3072]{3,2,1,0:T(8,128)} reshape(f32[6,64,8,384]{3,2,1,0:T(8,128)} %copy.75) | data formatting | bytes 9437184 | tf_op jit(solution)/shard_map/broadcast_in_dim | solution.py:172
  (103 shorter events, 27.1 us)
Async XLA Ops:
  7.2 1.3 copy-start.16
  7.2 242.9 %all-gather.3.cloned.1.call-start = ((), (), s32[]{:S(2)}) async-start(), calls=%async_computation.8 | async-start | bytes 10616832 | tf_op jit(solution)/shard_map/all_gather | solution.py:90
  17.0 7.5 %copy-start.7 = (bf16[1,6,64,3072]{3,2,1,0:T(8,128)(2,1)S(1)}, bf16[1,6,64,3072]{3,2,1,0:T(8,128)(2,1)}, u32[]{:S(2)}) copy-start(bf16[1,6,64,3072]{3,2,1,0:T(8,128)(2,1)} %param.16) | copy-start | bytes 7077892
  17.0 67.2 %all-to-all-start = ((bf16[8,2,36864]{2,1,0:T(2,128)(2,1)}), bf16[8,2,36864]{2,1,0:T(2,128)(2,1)S(1)}, u32[]{:S(2)}, u32[]{:S(2)}) async-start(bf16[8,2,36864]{2,1,0:T(2,128)(2,1)} %reshape.236), calls=%async_computation | async-start | bytes 2359296 | tf_op jit(solution)/shard_map/all_to_all | solution.py:99
  45.5 44.7 %copy-start.27 = (s32[48]{0:T(128)S(1)}, s32[48]{0:T(128)}, u32[]{:S(2)}) copy-start(s32[48]{0:T(128)} %param.19) | copy-start | bytes 580
  45.5 44.8 %copy-start.28 = (s32[8]{0:T(128)S(1)}, s32[8]{0:T(128)}, u32[]{:S(2)}) copy-start(s32[8]{0:T(128)} %param.18) | copy-start | bytes 100
  45.5 45.5 %copy-start.10 = (f32[128,3072]{1,0:T(8,128)S(1)}, f32[128,3072]{1,0:T(8,128)}, u32[]{:S(2)}) copy-start(f32[128,3072]{1,0:T(8,128)} %param.12) | copy-start | bytes 4718596
  84.2 1.0 copy-start.3
  85.2 115.8 %all-to-all-start.2 = ((bf16[8,2,73728]{2,1,0:T(2,128)(2,1)}), bf16[8,2,73728]{2,1,0:T(2,128)(2,1)}, u32[]{:S(2)}, u32[]{:S(2)}) async-start(bf16[8,2,73728]{2,1,0:T(2,128)(2,1)} %reshape.238), calls=%async_computation.2 | async-start | bytes 4718592 | tf_op jit(solution)/shard_map/all_to_all | solution.py:98
  90.4 0.5 copy-start.24
  99.3 110.6 %copy-start = (bf16[128,3072]{1,0:T(8,128)(2,1)S(1)}, bf16[128,3072]{1,0:T(8,128)(2,1)}, u32[]{:S(2)}) copy-start(bf16[128,3072]{1,0:T(8,128)(2,1)} %param.11) | copy-start | bytes 2359300
  200.9 30.7 %all-to-all-start.1 = ((bf16[8,64,192]{2,1,0:T(8,128)(2,1)}), bf16[8,64,192]{2,1,0:T(8,128)(2,1)S(1)}, u32[]{:S(2)}, u32[]{:S(2)}) async-start(bf16[8,64,192]{2,1,0:T(8,128)(2,1)} %gather_fusion), calls=%async_computation.1 | async-start | bytes 524288 | tf_op jit(solution)/shard_map/all_to_all | solution.py:103
  210.0 2.8 copy-start.29
  213.6 24.0 %copy-start.22 = (f32[128]{0:T(128)}, f32[128]{0:T(128)S(1)}, u32[]{:S(2)}) copy-start(f32[128]{0:T(128)S(1)} %fusion.20) | copy-start | bytes 1540
  228.5 9.2 %copy-start.1 = (f32[1,128,3072]{2,1,0:T(8,128)S(1)}, f32[1,128,3072]{2,1,0:T(8,128)}, u32[]{:S(2)}) copy-start(f32[1,128,3072]{2,1,0:T(8,128)} %get-tuple-element.7) | copy-start | bytes 4718596
  231.7 6.0 %copy-start.17 = (bf16[8,64,192]{2,1,0:T(8,128)(2,1)}, bf16[8,64,192]{2,1,0:T(8,128)(2,1)S(1)}, u32[]{:S(2)}) copy-start(bf16[8,64,192]{2,1,0:T(8,128)(2,1)S(1)} %all-to-all-done.1) | copy-start | bytes 589828
  231.7 17.1 %all-to-all-start.3 = ((bf16[8,64,384]{2,1,0:T(8,128)(2,1)}), bf16[8,64,384]{2,1,0:T(8,128)(2,1)S(1)}, u32[]{:S(2)}, u32[]{:S(2)}) async-start(bf16[8,64,384]{2,1,0:T(8,128)(2,1)} %gather_fusion.1), calls=%async_computation.3 | async-start | bytes 786432 | tf_op jit(solution)/shard_map/all_to_all | solution.py:102
  237.7 11.9 %copy-start.19 = (f32[1,3072]{1,0:T(1,128)S(1)}, f32[1,3072]{1,0:T(1,128)}, u32[]{:S(2)}) copy-start(f32[1,3072]{1,0:T(1,128)} %param.14) | copy-start | bytes 36868
  237.7 12.4 %copy-start.30 = (f32[128]{0:T(128)}, f32[128]{0:T(128)S(1)}, u32[]{:S(2)}) copy-start(f32[128]{0:T(128)S(1)} %add_rsqrt_fusion.1) | copy-start | bytes 1540
  241.3 17.0 %copy-start.8 = (bf16[64,1536]{1,0:T(8,128)(2,1)}, bf16[64,1536]{1,0:T(8,128)(2,1)S(1)}, u32[]{:S(2)}) copy-start(bf16[64,1536]{1,0:T(8,128)(2,1)S(1)} %reshape.210) | copy-start | bytes 589828
  248.8 0.7 copy-start.11
  250.1 5.4 copy-start.18
  250.1 5.3 copy-start.5
  250.1 8.5 %copy-start.2 = (bf16[1,3072,1536]{2,1,0:T(8,128)(2,1)S(1)}, bf16[1,3072,1536]{2,1,0:T(8,128)(2,1)}, u32[]{:S(2)}) copy-start(bf16[1,3072,1536]{2,1,0:T(8,128)(2,1)} %all-gather.3.cloned.1.call-done) | copy-start | bytes 28311556
  255.4 1.5 copy-start.13
  257.0 4.7 collective-permute-start
  258.6 3.1 copy-start.12
  258.7 3.1 copy-start.20
  261.8 0.9 copy-start.23
  264.7 4.6 copy-start.4
  264.7 4.6 collective-permute-start.1
  271.0 0.7 copy-start.14
  272.9 12.5 %copy-start.9 = (bf16[64,1536]{1,0:T(8,128)(2,1)S(1)}, bf16[64,1536]{1,0:T(8,128)(2,1)}, u32[]{:S(2)}) copy-start(bf16[64,1536]{1,0:T(8,128)(2,1)} %copy-done.8) | copy-start | bytes 589828
  272.9 12.5 %copy-start.21 = (f32[1,3072]{1,0:T(1,128)S(1)}, f32[1,3072]{1,0:T(1,128)}, u32[]{:S(2)}) copy-start(f32[1,3072]{1,0:T(1,128)} %param.14) | copy-start | bytes 36868
  272.9 12.5 %copy-start.26 = (f32[128]{0:T(128)S(1)}, f32[128]{0:T(128)}, u32[]{:S(2)}) copy-start(f32[128]{0:T(128)} %get-tuple-element.11) | copy-start | bytes 1540
  272.9 12.5 %copy-start.31 = (f32[128]{0:T(128)S(1)}, f32[128]{0:T(128)}, u32[]{:S(2)}) copy-start(f32[128]{0:T(128)} %copy-done.30) | copy-start | bytes 1540
  280.0 5.4 %copy-start.15 = (bf16[128,1536]{1,0:T(8,128)(2,1)S(1)}, bf16[128,1536]{1,0:T(8,128)(2,1)}, u32[]{:S(2)}) copy-start(bf16[128,1536]{1,0:T(8,128)(2,1)} %copy-done.14) | copy-start | bytes 1179652
  281.3 24.8 %all-to-all-start.6 = ((f32[8,1,12288]{2,1,0:T(1,128)}), f32[8,1,12288]{2,1,0:T(1,128)}, u32[]{:S(2)}, u32[]{:S(2)}) async-start(f32[8,1,12288]{2,1,0:T(1,128)} %reshape.242), calls=%async_computation.6 | async-start | bytes 786432 | tf_op jit(solution)/shard_map/all_to_all | solution.py:147
  306.0 26.6 %all-to-all-start.4 = ((f32[8,1,24576]{2,1,0:T(1,128)}), f32[8,1,24576]{2,1,0:T(1,128)S(1)}, u32[]{:S(2)}, u32[]{:S(2)}) async-start(f32[8,1,24576]{2,1,0:T(1,128)} %reshape.240), calls=%async_computation.4 | async-start | bytes 1572864 | tf_op jit(solution)/shard_map/all_to_all | solution.py:146
  315.7 0.8 copy-start.25
  332.6 0.9 copy-start.6
  333.5 74.8 %all-to-all-start.7 = ((f32[48,64,192]{2,1,0:T(8,128)}), f32[48,64,192]{2,1,0:T(8,128)S(1)}, u32[]{:S(2)}, u32[]{:S(2)}) async-start(f32[48,64,192]{2,1,0:T(8,128)} %copy.79), calls=%async_computation.7 | async-start | bytes 6291456 | tf_op jit(solution)/shard_map/all_to_all | solution.py:170
  408.3 108.7 %all-to-all-start.5 = ((f32[48,64,384]{2,1,0:T(8,128)}), f32[48,64,384]{2,1,0:T(8,128)}, u32[]{:S(2)}, u32[]{:S(2)}) async-start(f32[48,64,384]{2,1,0:T(8,128)} %copy.74), calls=%async_computation.5 | async-start | bytes 9437184 | tf_op jit(solution)/shard_map/all_to_all | solution.py:169
Sparse Core Ops, SparseCore 0:
  10.2 214.9 all-gather.2
where the time goes:
time: 547 us; the launch traced here: 537 us
  waiting for transfers between devices  307 us (56%)
  local copies, waits for them, and re-layouts  107 us (20%)
  starting transfers between devices  48.9 us (9%)
  other arithmetic  36.5 us (7%)
  matrix products  21.4 us (4%)
  between operations  16.4 us (3%)
    all_to_all x1, waiting for transfers between devices, body(): lax.all_to_all(down_factors[0], 'dp', split_axis=2, concat_axis=0, tiled=...  98.8 us
    all_to_all x1, waiting for transfers between devices, body(): lax.all_to_all(slot_down, 'dp', split_axis=0, concat_axis=2, tiled=True)  96 us
    unnamed x78, local copies, waits for them, and re-layouts  54.6 us
    all_to_all x1, waiting for transfers between devices, body(): lax.all_to_all(slot_up, 'dp', split_axis=0, concat_axis=2, tiled=True)  52.5 us
    all_to_all x1, waiting for transfers between devices, body(): lax.all_to_all(up_factors[0], 'dp', split_axis=2, concat_axis=0, tiled=True)  38.7 us
    unnamed x2, other arithmetic  20.7 us
    all_to_all x1, waiting for transfers between devices, body(): lax.all_to_all(sum_down, 'dp', split_axis=2, concat_axis=0, tiled=True)  11.2 us
  transfers between devices with their start and end apart: 11, of which 7 were waited for; matrix products, arithmetic and copies ran while one was open for 24% of the time, Pallas kernels for 0%

commit v1 on v0

--- a/solution.py
+++ b/solution.py
@@ -1,6 +1,8 @@
 import jax
 import jax.numpy as jnp
 from jax import lax
+from jax.experimental import pallas as pl
+from jax.experimental.pallas import tpu as pltpu
 from jax.sharding import PartitionSpec as P
 
 epsilon = 1e-06
@@ -66,7 +68,7 @@
     return (carried, lower_gradient, grad_upper)
 
 
-def body(
+def spread_body(
     latents,
     out_grad,
     frozen_weight,
@@ -172,6 +174,582 @@
     return (owned_down[None], owned_up[None])
 
 
+def swapped(value):
+    return lax.ppermute(value, "section", [(0, 1), (1, 0)])
+
+
+def ring_place(index, count):
+    return jnp.where(index % 2 == 0, index // 2, count - 1 - index // 2)
+
+
+def ring_member(place, count):
+    place = place % count
+    return jnp.where(place < count // 2, 2 * place, 2 * (count - 1 - place) + 1)
+
+
+def ring_pairs(groups, count, sign):
+    order = [*range(0, count, 2), *range(count - 1, 0, -2)]
+    pairs = []
+    for group in range(groups):
+        for place in range(count):
+            for core in range(2):
+                step = sign if core == 0 else -sign
+                source = (group * count + order[place]) * 2 + core
+                target = (group * count + order[(place + step) % count]) * 2 + core
+                pairs.append((source, target))
+    return pairs
+
+
+LANES = 128
+CHUNK = 16
+
+
+def product(left, right, contract):
+    dims = ((contract[:1], contract[1:]), ((), ()))
+    return lax.dot_general(left, right, dims, preferred_element_type=jnp.float32)
+
+
+def slot_columns(slot, rank, columns):
+    column = lax.broadcasted_iota(jnp.int32, (1, columns), 1)
+    return (column >= slot * rank) & (column < (slot + 1) * rank)
+
+
+def whole(memory_space=pltpu.VMEM):
+    return pl.BlockSpec(memory_space=memory_space)
+
+
+def call(kernel, outs, args, spaces, scratch=(), flops=0, out_spaces=None):
+    moved = sum(a.size * a.dtype.itemsize for a in (*args, *outs))
+    single = not isinstance(outs, (tuple, list))
+    return pl.pallas_call(
+        kernel,
+        out_shape=outs,
+        in_specs=[whole(space) for space in spaces],
+        out_specs=[whole(out_spaces[i] if out_spaces else pltpu.VMEM) for i in range(len(outs))],
+        scratch_shapes=list(scratch),
+        cost_estimate=pl.CostEstimate(flops=flops, bytes_accessed=moved, transcendentals=0),
+    )(*args)
+
+
+def shaped(dtype, *shape):
+    return jax.ShapeDtypeStruct(shape, dtype)
+
+
+def contribution_kernel(sizes, rank, *refs):
+    count = len(sizes)
+    scalars = refs[0]
+    lats, deltas = refs[1 : 1 + count], refs[1 + count : 1 + 2 * count]
+    gain_0, gain_1 = refs[1 + 2 * count : 3 + 2 * count]
+    sources = refs[3 + 2 * count : 9 + 2 * count]
+    update, head, inner, keep, give = refs[9 + 2 * count : 14 + 2 * count]
+    normed, tail, delta, slice_1, *held, sems = refs[14 + 2 * count :]
+    f32, bf16 = jnp.float32, jnp.bfloat16
+    core, offset = scalars[0], pl.multiple_of(scalars[1], LANES)
+    out_width = update.shape[1]
+    width = normed.shape[1]
+    own_columns = slice_1.shape[1]
+    columns = held[0].shape[0]
+    total = sum(sizes)
+
+    def copies(swap):
+        order = [sources[(i + 3) % 6] for i in range(6)] if swap else sources
+        return [pltpu.make_async_copy(order[i], held[i], sems.at[i]) for i in range(6)]
+
+    @pl.when(core == 0)
+    def _():
+        for copy in copies(False):
+            copy.start()
+
+    @pl.when(core != 0)
+    def _():
+        for copy in copies(True):
+            copy.start()
+
+    waits = copies(False)
+    begin = 0
+    for index, size in enumerate(sizes):
+        lat, grad = lats[index], deltas[index]
+        from_row = core * size if lat.shape[0] != size else 0
+
+        def rows_step(step, carry, lat=lat, grad=grad, from_row=from_row, begin=begin):
+            source = pl.ds(pl.multiple_of(from_row + step * CHUNK, CHUNK), CHUNK)
+            target = pl.ds(pl.multiple_of(begin + step * CHUNK, CHUNK), CHUNK)
+            values = lat[source, :].astype(f32)
+            inverse = lax.rsqrt(jnp.mean(values * values, axis=1, keepdims=True) + epsilon)
+            normed[target, :] = (values * inverse * gain_0[...]).astype(bf16)
+            tail[target, :] = (values[:, out_width:] * gain_1[:, out_width:]).astype(bf16)
+            delta[target, :] = grad[source, :]
+            slice_1[target, :] = lat[source, pl.ds(offset, own_columns)].astype(f32) * gain_1[
+                :, pl.ds(offset, own_columns)
+            ]
+            far = jnp.where(core == 0, 1, 0)
+
+            @pl.when(core == 0)
+            def _():
+                give[target, : width - out_width] = lat[source, out_width:]
+
+            @pl.when(core != 0)
+            def _():
+                keep[target, : width - out_width] = lat[source, out_width:]
+
+            return carry
+
+        lax.fori_loop(0, size // CHUNK, rows_step, 0)
+        begin += size
+
+    row = lax.broadcasted_iota(jnp.int32, (total, 1), 0)
+    slot = jnp.zeros((total, 1), jnp.int32) + scalars[2]
+    begin = sizes[0]
+    for index in range(1, count):
+        slot = jnp.where(row >= begin, scalars[2 + index], slot)
+        begin += sizes[index]
+    column = lax.broadcasted_iota(jnp.int32, (total, columns), 1)
+    mask = (column >= slot * rank) & (column < (slot + 1) * rank)
+
+    down_0, up_0, frozen_0, down_1, up_1, frozen_1 = held
+    waits[0].wait()
+    low = jnp.where(mask, product(normed[...], down_0[...], (1, 1)), 0.0).astype(bf16)
+    waits[1].wait()
+    waits[2].wait()
+    update[...] = (
+        product(normed[:, pl.ds(offset, own_columns)], frozen_0[...], (1, 0))
+        + product(low, up_0[...], (1, 0))
+    ).astype(update.dtype)
+    waits[4].wait()
+    low_grad = jnp.where(mask, product(delta[...], up_1[...], (1, 1)), 0.0).astype(bf16)
+    waits[5].wait()
+    slab = product(delta[...], frozen_1[...], (1, 1))
+    waits[3].wait()
+    head[...] = product(low_grad, down_1[:, :out_width], (1, 0))
+    tail_low = product(tail[...], down_1[:, out_width:], (1, 1))
+    inner_low = jnp.sum(low_grad.astype(f32) * tail_low, axis=1, keepdims=True)
+
+    @pl.when(offset < out_width)
+    def _():
+        head[:, pl.ds(offset, own_columns)] += slab
+        inner[...] = jnp.broadcast_to(inner_low, inner.shape)
+
+    @pl.when(offset >= out_width)
+    def _():
+        own = inner_low + jnp.sum(slice_1[...] * slab, axis=1, keepdims=True)
+        inner[...] = jnp.broadcast_to(own, inner.shape)
+
+    def fill(zeroth, oneth):
+        zeroth[:, :width] = normed[...]
+        zeroth[:, width:] = low
+        oneth[:, width - out_width : width] = delta[...]
+        oneth[:, width:] = low_grad
+
+    @pl.when(core == 0)
+    def _():
+        fill(keep, give)
+
+    @pl.when(core != 0)
+    def _():
+        fill(give, keep)
+
+
+def contribution(scalars, segments, gains, sources, slots, rank, out_width):
+    f32, bf16 = jnp.float32, jnp.bfloat16
+    sizes = tuple(size for _, _, size in segments)
+    total = sum(sizes)
+    columns, width = sources[0].shape
+    own_columns = sources[2].shape[0]
+    args = [scalars, *(s[0] for s in segments), *(s[1] for s in segments), *gains, *sources]
+    spaces = [pltpu.SMEM] + [pltpu.VMEM] * (2 * len(sizes) + 2) + [pl.ANY] * 6
+    outs = [
+        shaped(f32, total, out_width),
+        shaped(f32, total, out_width),
+        shaped(f32, total, LANES),
+        shaped(bf16, total, width + columns),
+        shaped(bf16, total, width + columns),
+    ]
+    scratch = [
+        pltpu.VMEM((total, width), bf16),
+        pltpu.VMEM((total, width - out_width), bf16),
+        pltpu.VMEM((total, out_width), bf16),
+        pltpu.VMEM((total, own_columns), f32),
+        *(pltpu.VMEM(sources[i % 3].shape, bf16) for i in range(6)),
+        pltpu.SemaphoreType.DMA((6,)),
+    ]
+    flops = 2 * total * columns * (2 * width + 3 * out_width) * 2
+    return call(
+        lambda *refs: contribution_kernel(sizes, rank, *refs), outs, args, spaces, scratch, flops
+    )
+
+
+def packed_inner(inner):
+    lane = lax.broadcasted_iota(jnp.int32, inner.shape, 1)
+    high = inner.astype(jnp.bfloat16)
+    low = (inner - high.astype(jnp.float32)).astype(jnp.bfloat16)
+    zero = jnp.zeros_like(high)
+    return jnp.where(lane == 0, high.astype(jnp.float32), jnp.where(lane == 1, low.astype(jnp.float32), 0.0)).astype(jnp.bfloat16)
+
+
+def unpacked_inner(value):
+    return jnp.sum(value.astype(jnp.float32), axis=1, keepdims=True)
+
+
+def chained(scalars, received, own, start, size, inner=None):
+    f32, bf16 = jnp.float32, jnp.bfloat16
+    got = received.shape[0] if received is not None else 0
+    rows = max(got, size)
+    out_width = own.shape[1]
+    extra = 0 if inner is None else LANES
+
+    def kernel(scalars, *refs):
+        refs = list(refs)
+        arrived = refs.pop(0) if got else None
+        own, inner = refs[0], (refs[1] if extra else None)
+        out = refs[-1]
+        core = scalars[0]
+
+        def step(index, carry):
+            base = index * CHUNK
+            target = pl.ds(pl.multiple_of(base, CHUNK), CHUNK)
+
+            def gather(wide, narrow):
+                total = wide
+                return total
+
+            low = core * (rows // 2)
+            inside = (base >= low) & (base < low + rows // 2)
+            local = jnp.where(inside, base - low, 0)
+            if got == 0:
+                main, extra_rows = own[pl.ds(pl.multiple_of(start + base, CHUNK), CHUNK), :], None
+                scalar = inner[pl.ds(pl.multiple_of(start + base, CHUNK), CHUNK), :] if extra else None
+            else:
+                full = got == rows and size == rows
+                at_got = base if got == rows else local
+                at_own = start + (base if size == rows else local)
+                theirs = arrived[pl.ds(pl.multiple_of(at_got, CHUNK), CHUNK), :].astype(f32)
+                ours = own[pl.ds(pl.multiple_of(at_own, CHUNK), CHUNK), :]
+                if extra:
+                    inner_ours = inner[pl.ds(pl.multiple_of(at_own, CHUNK), CHUNK), :]
+                    inner_theirs = jnp.sum(theirs[:, out_width:], axis=1, keepdims=True)
+                    theirs = theirs[:, :out_width]
+                if got != rows:
+                    theirs = jnp.where(inside, theirs, 0.0)
+                    if extra:
+                        inner_theirs = jnp.where(inside, inner_theirs, 0.0)
+                if size != rows:
+                    ours = jnp.where(inside, ours, 0.0)
+                    if extra:
+                        inner_ours = jnp.where(inside, inner_ours, 0.0)
+                main = theirs + ours
+                scalar = inner_theirs + inner_ours if extra else None
+            out[target, :out_width] = main.astype(bf16)
+            if extra:
+                out[target, out_width:] = packed_inner(scalar)
+            return carry
+
+        lax.fori_loop(0, rows // CHUNK, step, 0)
+
+    args = [scalars, *([received] if got else []), own, *([inner] if extra else [])]
+    spaces = [pltpu.SMEM] + [pltpu.VMEM] * (len(args) - 1)
+    return call(kernel, [shaped(bf16, rows, out_width + extra)], args, spaces)[0]
+
+
+def owner_kernel(scalars, scales, update_a, update_b, head_a, head_b, lat, grad, gain_1, head_next, delta_0):
+    f32, bf16 = jnp.float32, jnp.bfloat16
+    rows, out_width = head_next.shape
+    width = lat.shape[1]
+    scale_0, fill = scales[0], scalars[1]
+
+    def step(index, carry):
+        at = pl.ds(pl.multiple_of(index * CHUNK, CHUNK), CHUNK)
+        values = lat[at, :].astype(f32)
+        update = update_a[at, :].astype(f32) + update_b[at, :].astype(f32)
+        new = (values[:, :out_width] + scale_0 * update).astype(bf16)
+        head_next[at, :] = new
+        new = new.astype(f32)
+        tail = values[:, out_width:]
+        total = jnp.sum(new * new, axis=1, keepdims=True) + jnp.sum(tail * tail, axis=1, keepdims=True)
+        inverse = lax.rsqrt(total / width + epsilon)
+        slope = head_a[at, :].astype(f32) + head_b[at, :].astype(f32)
+        scaled = gain_1[:, :out_width] * slope[:, :out_width]
+        inner = jnp.sum(new * scaled, axis=1, keepdims=True) + jnp.sum(slope[:, out_width:], axis=1, keepdims=True)
+        cubed = inverse * inverse * inverse
+        row = lax.broadcasted_iota(jnp.int32, (CHUNK, 1), 0) + index * CHUNK
+        top = jnp.where(row < fill, grad[at, :], 0.0)
+        carried = (top + (inverse * scaled - new * (cubed * (inner / width)))).astype(bf16)
+        delta_0[at, :] = (scale_0 * carried.astype(f32)).astype(bf16)
+        return carry
+
+    lax.fori_loop(0, rows // CHUNK, step, 0)
+
+
+def gradient_kernel(sizes, rank, *refs):
+    f32, bf16 = jnp.float32, jnp.bfloat16
+    batches = len(sizes)
+    hops = batches
+    take = iter(refs)
+    scalars, gain_1 = next(take), next(take)
+    keeps = [next(take) for _ in range(batches)]
+    gots = [next(take) for _ in range(batches)]
+    head_own, delta_own = next(take), next(take)
+    heads = [next(take) for _ in range(hops)]
+    deltas = [next(take) for _ in range(hops)]
+    lates = [next(take) for _ in range(hops)]
+    down, up = next(take), next(take)
+    grad_down, grad_up = next(take), next(take)
+    normed, low_grad, low, delta, head, out_down, out_up, sems, out_sems = take
+    core = scalars[0]
+    rows, width = normed.shape
+    out_width = delta.shape[1]
+    half = head_own.shape[0] // 2
+    tail_width = width - out_width
+    piece = [half, *(each.shape[0] for each in heads)]
+    block_slots = [scalars[2 + i] for i in range(2 * len(piece))]
+
+    def batch_copies(first_layer):
+        copies = []
+        begin = 0
+        for side in (keeps, gots):
+            for source in side:
+                size = source.shape[0]
+                at = pl.ds(begin, size)
+                if first_layer:
+                    parts = [(source.at[:, pl.ds(0, width)], normed.at[at]), (source.at[:, pl.ds(width, source.shape[1] - width)], low.at[at])]
+                else:
+                    parts = [
+                        (source.at[:, pl.ds(0, tail_width)], normed.at[at, pl.ds(out_width, tail_width)]),
+                        (source.at[:, pl.ds(tail_width, out_width)], delta.at[at]),
+                        (source.at[:, pl.ds(width, source.shape[1] - width)], low_grad.at[at]),
+                    ]
+                copies += parts
+                begin += size
+        return copies
+
+    def piece_copies(first_layer):
+        copies = []
+        begin = 0
+        target = delta if first_layer else head
+        mine = deltas if first_layer else heads
+        own = delta_own if first_layer else head_own
+        for side in (0, 1):
+            start = half * (core if side == 0 else 1 - core)
+            copies.append((own.at[pl.ds(pl.multiple_of(start, CHUNK), half)], target.at[pl.ds(begin, half)]))
+            begin += half
+            for source in mine if side == 0 else lates:
+                copies.append((source, target.at[pl.ds(begin, source.shape[0])]))
+                begin += source.shape[0]
+        return copies
+
+    def started(pairs):
+        copies = [pltpu.make_async_copy(a, b, sems.at[i]) for i, (a, b) in enumerate(pairs)]
+        for copy in copies:
+            copy.start()
+        return copies
+
+    def masked(value, out):
+        begin = 0
+        for slot, size in zip(block_slots, piece * 2):
+            at = slice(begin, begin + size)
+            out[at, :] = jnp.where(slot_columns(slot, rank, out.shape[1]), value[at], 0.0).astype(bf16)
+            begin += size
+
+    @pl.when(core == 0)
+    def _():
+        copies = started(piece_copies(True) + batch_copies(True))
+        for copy in copies[: 2 * len(piece)]:
+            copy.wait()
+        masked(product(delta[...], up[...], (1, 1)), low_grad)
+        for copy in copies[2 * len(piece) :]:
+            copy.wait()
+
+    @pl.when(core != 0)
+    def _():
+        copies = started(piece_copies(False) + batch_copies(False))
+        for copy in copies:
+            copy.wait()
+
+        def step(index, carry):
+            at = pl.ds(pl.multiple_of(index * CHUNK, CHUNK), CHUNK)
+            new, old = head[at, :].astype(f32), normed[at, out_width:].astype(f32)
+            total = jnp.sum(new * new, axis=1, keepdims=True) + jnp.sum(old * old, axis=1, keepdims=True)
+            inverse = lax.rsqrt(total / width + epsilon)
+            normed[at, :out_width] = (new * inverse * gain_1[:, :out_width]).astype(bf16)
+            normed[at, out_width:] = (old * inverse * gain_1[:, out_width:]).astype(bf16)
+            return carry
+
+        lax.fori_loop(0, rows // CHUNK, step, 0)
+        masked(product(normed[...], down[...], (1, 1)), low)
+
+    copies = []
+    for left, right, out, target in ((low_grad, normed, out_down, grad_down), (low, delta, out_up, grad_up)):
+        turned = left[...].T
+        tile = 512
+        for at in range(0, out.shape[1], tile):
+            span = pl.ds(at, tile)
+            out[:, span] = product(turned, right[:, span], (1, 0))
+            copy = pltpu.make_async_copy(out.at[:, span], target.at[:, span], out_sems.at[len(copies)])
+            copy.start()
+            copies.append(copy)
+    for copy in copies:
+        copy.wait()
+
+
+def ring_body(
+    latents,
+    out_grad,
+    frozen_weight,
+    norm_gain,
+    time_gate,
+    down_factors,
+    up_factors,
+    block_jobs,
+    owners,
+    block_steps,
+    block_fill,
+):
+    f32, bf16 = jnp.float32, jnp.bfloat16
+    core = lax.axis_index("section")
+    member = lax.axis_index("dp")
+    count = lax.axis_size("dp")
+    rows, width = latents.shape
+    half = rows // 2
+    slots, rank = down_factors.shape[1:3]
+    columns = slots * rank
+    out_width = up_factors.shape[3]
+    own_columns = frozen_weight.shape[1]
+    first = core == 0
+    place = ring_place(member, count)
+    away = ring_pairs(lax.axis_size("groups"), count, 1)
+    back = ring_pairs(lax.axis_size("groups"), count, -1)
+    axes = ("groups", "dp", "section")
+    outward = lambda value: lax.ppermute(value, axes, away)
+    inward = lambda value: lax.ppermute(value, axes, back)
+    reach = count // 2
+
+    small = jnp.concatenate([norm_gain[0], time_gate[0]])
+    small_in = swapped(small)
+    small_0 = jnp.where(first, small, small_in)
+    small_1 = jnp.where(first, small_in, small)
+    gain_0, gain_1 = small_0[None, :width], small_1[None, :width]
+    chosen = block_steps[0] == jnp.arange(time_gate.shape[1], dtype=jnp.int32)
+    scale_0 = jnp.sum(jnp.where(chosen, small_0[width:], 0.0))
+    scale_1 = jnp.sum(jnp.where(chosen, small_1[width:], 0.0))
+    live = jnp.arange(rows, dtype=jnp.int32)[:, None] < block_fill[0]
+    delta_1 = (scale_1 * jnp.where(live, out_grad[:, :out_width], 0.0)).astype(bf16)
+
+    def halved(value):
+        return lax.dynamic_slice(value, (core * half, 0), (half, value.shape[1]))
+
+    def spread(value):
+        arrived = []
+        for hop in range(1, reach + 1):
+            value = outward(halved(value) if hop == reach else value)
+            arrived.append(value)
+        return arrived
+
+    lat_near, delta_near = spread(latents), spread(delta_1)
+
+    down, up = down_factors[0].reshape(columns, width), up_factors[0].reshape(columns, out_width)
+    frozen = frozen_weight[0]
+    sources = [down, up, frozen, *map(swapped, (down, up, frozen))]
+
+    matches = block_jobs[:, None] == jnp.arange(owners.shape[0], dtype=jnp.int32)[None, :]
+    slot_of = jnp.sum(jnp.where(matches, owners[None, :], 0), axis=1) - member * slots
+    steps = jnp.arange(reach + 1, dtype=jnp.int32)
+    toward = jnp.where(first, -1, 1)
+    blocks = ring_member(jnp.concatenate([place + toward * steps, place - toward * steps]), count)
+    picked = blocks[:, None] == jnp.arange(count, dtype=jnp.int32)[None, :]
+    block_slots = jnp.sum(jnp.where(picked, slot_of[None, :], 0), axis=1)
+
+    def listed(*values):
+        return jnp.stack([jnp.asarray(value, jnp.int32) for value in values])
+
+    offset = member * own_columns
+    gains = (gain_0, gain_1)
+
+    def contributed(scalars, segments):
+        return contribution(scalars, segments, gains, sources, slots, rank, out_width)
+
+    head_scalars = listed(core, offset)
+    all_scalars = jnp.concatenate([head_scalars, block_slots])
+    near = [
+        contributed(
+            all_scalars,
+            [(latents, delta_1, half), (lat_near[0], delta_near[0], rows)],
+        )
+    ]
+    for hop in range(2, reach + 1):
+        lat, delta = lat_near[hop - 1], delta_near[hop - 1]
+        scalars = jnp.concatenate([head_scalars, block_slots[hop : hop + 1]])
+        near.append(contributed(scalars, [(lat, delta, lat.shape[0])]))
+    gots = [swapped(each[4]) for each in near]
+
+    starts = [(0, half), *((half if hop == 1 else 0, rows) for hop in range(1, reach)), (0, half)]
+    update_in = head_in = None
+    for hop in range(reach, -1, -1):
+        update, head, inner = near[max(hop - 1, 0)][:3]
+        start, size = starts[hop]
+        update_out = chained(head_scalars, update_in, update, start, size)
+        head_out = chained(head_scalars, head_in, head, start, size, inner)
+        pass_on = inward if hop else swapped
+        update_in, head_in = pass_on(update_out), pass_on(head_out)
+    head_next, delta_0 = call(
+        owner_kernel,
+        [shaped(bf16, rows, out_width)] * 2,
+        [listed(core, block_fill[0]), scale_0[None], update_out, update_in, head_out, head_in, latents, out_grad[:, :out_width], gain_1],
+        [pltpu.SMEM] * 2 + [pltpu.VMEM] * 7,
+    )
+
+    head_near, delta_0_near = spread(head_next), spread(delta_0)
+    lates = [swapped(jnp.where(first, a, b)) for a, b in zip(head_near, delta_0_near)]
+
+    sizes = [each[3].shape[0] for each in near]
+    total = 2 * sum(sizes)
+    args = [all_scalars, gain_1, *(each[3] for each in near), *gots, head_next, delta_0, *head_near, *delta_0_near, *lates, down, up]
+    spaces = [pltpu.SMEM, pltpu.VMEM] + [pl.ANY] * (len(args) - 4) + [pltpu.VMEM] * 2
+    grad_down, grad_up = call(
+        lambda *refs: gradient_kernel(sizes, rank, *refs),
+        [shaped(f32, columns, width), shaped(f32, columns, out_width)],
+        args,
+        spaces,
+        [
+            pltpu.VMEM((total, width), bf16),
+            pltpu.VMEM((total, columns), bf16),
+            pltpu.VMEM((total, columns), bf16),
+            pltpu.VMEM((total, out_width), bf16),
+            pltpu.VMEM((total, out_width), bf16),
+            pltpu.VMEM((columns, width), f32),
+            pltpu.VMEM((columns, out_width), f32),
+            pltpu.SemaphoreType.DMA((2 * (reach + 1) + 6 * reach,)),
+            pltpu.SemaphoreType.DMA(((width + out_width) // 512,)),
+        ],
+        flops=2 * total * columns * (width + 2 * out_width),
+        out_spaces=[pl.ANY, pl.ANY],
+    )
+    return (
+        grad_down.reshape(1, slots, rank, width),
+        grad_up.reshape(1, slots, rank, out_width),
+    )
+
+
+def body(*arrays):
+    latents, up_factors, block_fill = arrays[0], arrays[6], arrays[10]
+    count = lax.axis_size("dp")
+    rows, width = latents.shape
+    out_width = up_factors.shape[3]
+    own_columns = arrays[2].shape[1]
+    gathered = count * rows * (2 * width + 4 * out_width) * 2
+    fits = (
+        block_fill.shape[0] == 1
+        and count % 2 == 0
+        and count >= 4
+        and rows % 32 == 0
+        and width % 512 == 0
+        and out_width % 512 == 0
+        and own_columns % 128 == 0
+        and out_width % own_columns == 0
+        and lax.axis_size("section") == 2
+        and gathered <= 48 * 2**20
+    )
+    return ring_body(*arrays) if fits else spread_body(*arrays)
+
+
 def solution(mesh):
     placed = (
         P(("groups", "dp"), None),

time: 547 us -> 212 us (0.39)
  the two profiles are of different devices: /device:TPU:0 before, /device:TPU:1 now
where the time goes in v1:
time: 212 us; the launch traced here: 211 us
  Pallas kernels  86.5 us (41%)
  waiting for transfers between devices  51 us (24%)
  starting transfers between devices  42.5 us (20%)
  local copies, waits for them, and re-layouts  14.9 us (7%)
  other arithmetic  14 us (7%)
  between operations  2.5 us (1%)
    pallas_call x16, Pallas kernels, call(): pl.pallas_call(kernel, out_shape=outs, in_specs=[whole(space) for space i...  86.5 us
    ppermute x16, waiting for transfers between devices, ring_body(): outward = lambda value: lax.ppermute(value, axes, away)  45.3 us
    ppermute x14, starting transfers between devices, swapped(): return lax.ppermute(value, 'section', [(0, 1), (1, 0)])  23.4 us
    ppermute x16, starting transfers between devices, ring_body(): outward = lambda value: lax.ppermute(value, axes, away)  13 us
    unnamed x68, local copies, waits for them, and re-layouts  10.4 us
    ppermute x8, starting transfers between devices, ring_body(): inward = lambda value: lax.ppermute(value, axes, back)  6.06 us
  transfers between devices with their start and end apart: 38, of which 15 were waited for; matrix products, arithmetic and copies ran while one was open for 9% of the time, Pallas kernels for 24%

profile of v1, /device:TPU:1, one launch (start us, length us, event | category | flops | bytes accessed | tf_op | source)
XLA Modules:
  0.0 211.4 jit_solution(4604295921724105769)
XLA Ops:
  0.6 2.1 collective-permute-start.1
  8.3 4.5 %collective-permute-done.1.refs_2_ = bf16[128,3072]{1,0:T(8,128)(2,1)} collective-permute-done((bf16[128,3072]{1,0:T(8,128)(2,1)}, bf16[128,3072]{1,0:T(8,128)(2,1)}, u32[]{:S(2)}, u32[]{:S(2)}) %collective-permute-start.1) | collective-permute-done | bytes 786464 | tf_op jit(solution)/shard_map/ppermute | solution.py:621
  12.8 1.4 collective-permute-start.6
  14.2 2.8 %fusion.5 = (f32[128,1536]{1,0:T(8,128)}, bf16[128,1536]{1,0:T(8,128)(2,1)}) fusion(f32[128,3072]{1,0:T(8,128)} %param.12, pred[128]{0:T(512)(128)(4,1)} %iota_compare_fusion.2, f32[]{:T(128)} %fusion), kind=kLoop, calls=%fused_computation.37 | loop fusion | flops 589824 | bytes 1966212 | tf_op jit(solution)/shard_map/slice | solution.py:634
  17.0 1.3 collective-permute-start.2
  18.3 2.2 %collective-permute-start.4 = (bf16[384,1536]{1,0:T(8,128)(2,1)}, bf16[384,1536]{1,0:T(8,128)(2,1)}, u32[]{:S(2)}, u32[]{:S(2)}) collective-permute-start(bf16[384,1536]{1,0:T(8,128)(2,1)} %bitcast.28), channel_id=1, source_target_pairs={{0,1},{1,0},{2,3},{3,2},{4,5},{5,4},{6,7},{7,6},{8,9},{9,8},{10,11... | collective-permute-start | bytes 3538952 | tf_op jit(solution)/shard_map/ppermute | solution.py:178
  20.5 3.8 %collective-permute-done.6.refs_1_ = bf16[128,3072]{1,0:T(8,128)(2,1)} collective-permute-done((bf16[128,3072]{1,0:T(8,128)(2,1)}, bf16[128,3072]{1,0:T(8,128)(2,1)}, u32[]{:S(2)}, u32[]{:S(2)}) %collective-permute-start.6) | collective-permute-done | bytes 786464 | tf_op jit(solution)/shard_map/ppermute | solution.py:621
  24.3 1.4 collective-permute-start.8
  26.5 2.0 collective-permute-done.2.refs_4_
  28.5 1.4 collective-permute-start.7
  31.2 9.9 %collective-permute-done.7.refs_2_ = bf16[128,1536]{1,0:T(8,128)(2,1)} collective-permute-done((bf16[128,1536]{1,0:T(8,128)(2,1)}, bf16[128,1536]{1,0:T(8,128)(2,1)}, u32[]{:S(2)}, u32[]{:S(2)}) %collective-permute-start.7) | collective-permute-done | bytes 393248 | tf_op jit(solution)/shard_map/ppermute | solution.py:621
  41.1 1.4 collective-permute-start.9
  44.1 1.3 collective-permute-start.10
  45.5 2.9 %collective-permute-done.9.refs_2_ = bf16[128,1536]{1,0:T(8,128)(2,1)} collective-permute-done((bf16[128,1536]{1,0:T(8,128)(2,1)}, bf16[128,1536]{1,0:T(8,128)(2,1)}, u32[]{:S(2)}, u32[]{:S(2)}) %collective-permute-start.9) | collective-permute-done | bytes 393248 | tf_op jit(solution)/shard_map/ppermute | solution.py:621
  49.3 1.4 collective-permute-start.11
  52.6 1.3 slice.33
  56.1 7.7 %shard_map.125 = (f32[64,1536]{1,0:T(8,128)}, f32[64,1536]{1,0:T(8,128)}, f32[64,128]{1,0:T(8,128)}, bf16[64,3456]{1,0:T(8,128)(2,1)}, bf16[64,3456]{1,0:T(8,128)(2,1)}) custom-call(s32[3]{0:T(128)} %pad_add_fusion.4.refs_0_, bf16[64,3072]{1,0:T(8,128)(2,1)} %collective-permute-done.10.refs_1_, bf16[64,1536]{1,0:T(8,128)(2,1)} %copy-done.20, ...), custom_call_target="tpu_custom_call" | custom-call | flops 1056964608 | bytes 11755532 | tf_op jit(solution)/shard_map/pallas_call | solution.py:224
  63.9 1.8 shard_map.131
  65.6 1.5 collective-permute-start.21
  68.3 1.7 shard_map.126
  70.0 1.4 collective-permute-start.16
  71.4 9.0 %shard_map.124 = (f32[128,1536]{1,0:T(8,128)}, f32[128,1536]{1,0:T(8,128)}, f32[128,128]{1,0:T(8,128)}, bf16[128,3456]{1,0:T(8,128)(2,1)}, bf16[128,3456]{1,0:T(8,128)(2,1)}) custom-call(s32[3]{0:T(128)} %pad_add_fusion.3.refs_0_, bf16[128,3072]{1,0:T(8,128)(2,1)} %collective-permute-done.8.refs_1_, bf16[128,1536]{1,0:T(8,128)(2,1)} %collective-permute-done.9.refs_2_, ...), custom_call_target="tpu_custom_call" | custom-call | flops 2113929216 | bytes 14049292 | tf_op jit(solution)/shard_map/pallas_call | solution.py:224
  81.1 2.7 %shard_map.132 = bf16[128,1664]{1,0:T(8,128)(2,1)} custom-call(s32[2]{0:T(128)} %pad_add_fusion.6.scalars, bf16[64,1664]{1,0:T(8,128)(2,1)} %copy-done.16, f32[128,1536]{1,0:T(8,128)} %get-tuple-element.40.refs_1_, f32[128,128]{1,0:T(8,128)} %get-tuple-element.41.refs_2_), custom_call_target="tpu_custom_call" | custom-call | bytes 1490952 | tf_op jit(solution)/shard_map/pallas_call | solution.py:224
  85.8 2.2 %shard_map.127 = bf16[128,1536]{1,0:T(8,128)(2,1)} custom-call(s32[2]{0:T(128)} %pad_add_fusion.6.scalars, bf16[64,1536]{1,0:T(8,128)(2,1)} %copy-done.17, f32[128,1536]{1,0:T(8,128)} %get-tuple-element.35.refs_1_), custom_call_target="tpu_custom_call" | custom-call | bytes 1376264 | tf_op jit(solution)/shard_map/pallas_call | solution.py:224
  87.9 1.3 collective-permute-start.17
  90.5 8.9 %shard_map.123 = (f32[128,1536]{1,0:T(8,128)}, f32[128,1536]{1,0:T(8,128)}, f32[128,128]{1,0:T(8,128)}, bf16[128,3456]{1,0:T(8,128)(2,1)}, bf16[128,3456]{1,0:T(8,128)(2,1)}) custom-call(s32[3]{0:T(128)} %pad_add_fusion.1.refs_0_, bf16[128,3072]{1,0:T(8,128)(2,1)} %collective-permute-done.6.refs_1_, bf16[128,1536]{1,0:T(8,128)(2,1)} %collective-permute-done.7.refs_2_, ...), custom_call_target="tpu_custom_call" | custom-call | flops 2113929216 | bytes 14049292 | tf_op jit(solution)/shard_map/pallas_call | solution.py:224
  100.2 2.7 %shard_map.133 = bf16[128,1664]{1,0:T(8,128)(2,1)} custom-call(s32[2]{0:T(128)} %pad_add_fusion.6.scalars, bf16[128,1664]{1,0:T(8,128)(2,1)} %copy-done.6, f32[128,1536]{1,0:T(8,128)} %get-tuple-element.42.refs_1_, f32[128,128]{1,0:T(8,128)} %get-tuple-element.43.refs_2_), custom_call_target="tpu_custom_call" | custom-call | bytes 1703944 | tf_op jit(solution)/shard_map/pallas_call | solution.py:224
  103.9 2.1 shard_map.128
  106.8 10.1 %shard_map.122 = (f32[192,1536]{1,0:T(8,128)}, f32[192,1536]{1,0:T(8,128)}, f32[192,128]{1,0:T(8,128)}, bf16[192,3456]{1,0:T(8,128)(2,1)}, bf16[192,3456]{1,0:T(8,128)(2,1)}) custom-call(s32[12]{0:T(128)} %pad_add_fusion.refs_0_, bf16[128,3072]{1,0:T(8,128)(2,1)} %lat.1, bf16[128,3072]{1,0:T(8,128)(2,1)} %collective-permute-done.1.refs_2_, ...), custom_call_target="tpu_custom_call" | custom-call | flops 3170893824 | bytes 16932912 | tf_op jit(solution)/shard_map/pallas_call | solution.py:224
  117.6 2.9 %shard_map.134 = bf16[128,1664]{1,0:T(8,128)(2,1)} custom-call(s32[2]{0:T(128)} %pad_add_fusion.6.scalars, bf16[128,1664]{1,0:T(8,128)(2,1)} %copy-done.4, f32[192,1536]{1,0:T(8,128)} %get-tuple-element.44.refs_1_, f32[192,128]{1,0:T(8,128)} %get-tuple-element.45.refs_2_), custom_call_target="tpu_custom_call" | custom-call | bytes 2129928 | tf_op jit(solution)/shard_map/pallas_call | solution.py:224
  121.5 2.3 %shard_map.129 = bf16[128,1536]{1,0:T(8,128)(2,1)} custom-call(s32[2]{0:T(128)} %pad_add_fusion.6.scalars, bf16[128,1536]{1,0:T(8,128)(2,1)} %copy-done.12, f32[192,1536]{1,0:T(8,128)} %get-tuple-element.37.refs_1_), custom_call_target="tpu_custom_call" | custom-call | bytes 1966088 | tf_op jit(solution)/shard_map/pallas_call | solution.py:224
  123.8 3.9 %collective-permute-done.24.refs_0_ = bf16[128,1664]{1,0:T(8,128)(2,1)S(1)} collective-permute-done((bf16[128,1664]{1,0:T(8,128)(2,1)}, bf16[128,1664]{1,0:T(8,128)(2,1)S(1)}, u32[]{:S(2)}, u32[]{:S(2)}) %collective-permute-start.24) | collective-permute-done | bytes 426016 | tf_op jit(solution)/shard_map/ppermute | solution.py:622
  128.5 2.8 %shard_map.135.head_a = bf16[128,1664]{1,0:T(8,128)(2,1)} custom-call(s32[2]{0:T(128)} %pad_add_fusion.6.scalars, bf16[128,1664]{1,0:T(8,128)(2,1)} %copy-done.7, f32[192,1536]{1,0:T(8,128)} %get-tuple-element.44.refs_1_, f32[192,128]{1,0:T(8,128)} %get-tuple-element.45.refs_2_), custom_call_target="tpu_custom_call" | custom-call | bytes 2129928 | tf_op jit(solution)/shard_map/pallas_call | solution.py:224
  131.3 6.6 %collective-permute-start.25 = (bf16[128,1664]{1,0:T(8,128)(2,1)}, bf16[128,1664]{1,0:T(8,128)(2,1)S(1)}, u32[]{:S(2)}, u32[]{:S(2)}) collective-permute-start(bf16[128,1664]{1,0:T(8,128)(2,1)} %shard_map.135.head_a), channel_id=1, source_target_pairs={{0,1},{1,0},{2,3},{3,2},{4,5},{5,4},{6,7},{7,6},{8,9},{9,8},{10,11... | collective-permute-start | bytes 1277960 | tf_op jit(solution)/shard_map/ppermute | solution.py:178
  138.6 2.3 %shard_map.130.update_a = bf16[128,1536]{1,0:T(8,128)(2,1)} custom-call(s32[2]{0:T(128)} %pad_add_fusion.6.scalars, bf16[128,1536]{1,0:T(8,128)(2,1)} %copy-done.14, f32[192,1536]{1,0:T(8,128)} %get-tuple-element.37.refs_1_), custom_call_target="tpu_custom_call" | custom-call | bytes 1966088 | tf_op jit(solution)/shard_map/pallas_call | solution.py:224
  144.0 4.7 %shard_map.136 = (bf16[128,1536]{1,0:T(8,128)(2,1)}, bf16[128,1536]{1,0:T(8,128)(2,1)}) custom-call(s32[2]{0:T(128)} %pad_add_fusion.5.scalars, f32[1]{0:T(128)} %bitcast.11.scales, bf16[128,1536]{1,0:T(8,128)(2,1)} %shard_map.130.update_a, bf16[128,1536]{1,0:T(8,128)(2,1)} %copy-done.15, bf16[128,1664]{1,0:T(8,128)(2,1)} %shard_map.135.head_a, ...), custom_call_target="tpu_custom_call" | custom-call | bytes 4009996 | tf_op jit(solution)/shard_map/pallas_call | solution.py:224
  149.0 3.2 %collective-permute-start.14 = (bf16[128,3456]{1,0:T(8,128)(2,1)S(1)}, bf16[128,3456]{1,0:T(8,128)(2,1)S(1)}, u32[]{:S(2)}, u32[]{:S(2)}) collective-permute-start(bf16[128,3456]{1,0:T(8,128)(2,1)S(1)} %copy-done.25), channel_id=1, source_target_pairs={{0,1},{1,0},{2,3},{3,2},{4,5},{5,4},{6,7},{7,6},{8,9},{9,8},{10,11... | collective-permute-start | bytes 2654216 | tf_op jit(solution)/shard_map/ppermute | solution.py:178
  152.7 3.2 %collective-permute-done.30.refs_16_ = bf16[128,1536]{1,0:T(8,128)(2,1)S(1)} collective-permute-done((bf16[128,1536]{1,0:T(8,128)(2,1)}, bf16[128,1536]{1,0:T(8,128)(2,1)S(1)}, u32[]{:S(2)}, u32[]{:S(2)}) %collective-permute-start.30) | collective-permute-done | bytes 393248 | tf_op jit(solution)/shard_map/ppermute | solution.py:621
  156.0 4.0 %collective-permute-done.26.refs_12_ = bf16[128,1536]{1,0:T(8,128)(2,1)S(1)} collective-permute-done((bf16[128,1536]{1,0:T(8,128)(2,1)}, bf16[128,1536]{1,0:T(8,128)(2,1)S(1)}, u32[]{:S(2)}, u32[]{:S(2)}) %collective-permute-start.26) | collective-permute-done | bytes 393248 | tf_op jit(solution)/shard_map/ppermute | solution.py:621
  160.3 4.0 %collective-permute-done.31.refs_17_ = bf16[128,1536]{1,0:T(8,128)(2,1)S(1)} collective-permute-done((bf16[128,1536]{1,0:T(8,128)(2,1)S(1)}, bf16[128,1536]{1,0:T(8,128)(2,1)S(1)}, u32[]{:S(2)}, u32[]{:S(2)}) %collective-permute-start.31) | collective-permute-done | bytes 393248 | tf_op jit(solution)/shard_map/ppermute | solution.py:621
  164.4 4.0 %collective-permute-done.27.refs_13_ = bf16[128,1536]{1,0:T(8,128)(2,1)S(1)} collective-permute-done((bf16[128,1536]{1,0:T(8,128)(2,1)S(1)}, bf16[128,1536]{1,0:T(8,128)(2,1)S(1)}, u32[]{:S(2)}, u32[]{:S(2)}) %collective-permute-start.27) | collective-permute-done | bytes 393248 | tf_op jit(solution)/shard_map/ppermute | solution.py:621
  168.7 4.0 %collective-permute-done.32.refs_18_ = bf16[128,1536]{1,0:T(8,128)(2,1)S(1)} collective-permute-done((bf16[128,1536]{1,0:T(8,128)(2,1)S(1)}, bf16[128,1536]{1,0:T(8,128)(2,1)S(1)}, u32[]{:S(2)}, u32[]{:S(2)}) %collective-permute-start.32) | collective-permute-done | bytes 393248 | tf_op jit(solution)/shard_map/ppermute | solution.py:621
  174.0 2.9 %collective-permute-done.28.refs_14_ = bf16[128,1536]{1,0:T(8,128)(2,1)S(1)} collective-permute-done((bf16[128,1536]{1,0:T(8,128)(2,1)S(1)}, bf16[128,1536]{1,0:T(8,128)(2,1)S(1)}, u32[]{:S(2)}, u32[]{:S(2)}) %collective-permute-start.28) | collective-permute-done | bytes 393248 | tf_op jit(solution)/shard_map/ppermute | solution.py:621
  178.1 4.1 %collective-permute-start.34 = (bf16[128,1536]{1,0:T(8,128)(2,1)S(1)}, bf16[128,1536]{1,0:T(8,128)(2,1)S(1)}, u32[]{:S(2)}, u32[]{:S(2)}) collective-permute-start(bf16[128,1536]{1,0:T(8,128)(2,1)S(1)} %broadcast_select_fusion.2), channel_id=1, source_target_pairs={{0,1},{1,0},{2,3},{3,2},{4,5},{5,4},{6,7},{7,6},{8,9},{9,8},{10,11... | collective-permute-start | bytes 1179656 | tf_op jit(solution)/shard_map/ppermute | solution.py:178
  182.2 1.6 collective-permute-start.35
  183.8 2.4 %collective-permute-start.36 = (bf16[128,1536]{1,0:T(8,128)(2,1)S(1)}, bf16[128,1536]{1,0:T(8,128)(2,1)S(1)}, u32[]{:S(2)}, u32[]{:S(2)}) collective-permute-start(bf16[128,1536]{1,0:T(8,128)(2,1)S(1)} %broadcast_select_fusion), channel_id=1, source_target_pairs={{0,1},{1,0},{2,3},{3,2},{4,5},{5,4},{6,7},{7,6},{8,9},{9,8},{10,11... | collective-permute-start | bytes 1179656 | tf_op jit(solution)/shard_map/ppermute | solution.py:178
  186.4 1.4 collective-permute-done.37.refs_23_
  188.7 22.6 %shard_map.137 = (f32[384,3072]{1,0:T(8,128)}, f32[384,1536]{1,0:T(8,128)}) custom-call(s32[12]{0:T(128)} %pad_add_fusion.refs_0_, f32[1,3072]{1,0:T(1,128)} %bitcast.39, bf16[192,3456]{1,0:T(8,128)(2,1)} %get-tuple-element.26.refs_2_, bf16[128,3456]{1,0:T(8,128)(2,1)} %get-tuple-element.27.refs_3_, bf16[128,3456]{1,0:T(8,128)(2,1)} %get-tuple-element.28.refs_4_, ...), custom_call_target="tpu_custom_call" | custom-call | flops 4831838208 | bytes 22622256 | tf_op jit(solution)/shard_map/pallas_call | solution.py:224
  (140 shorter events, 32.1 us)
Async XLA Ops:
  0.6 19.9 %copy-start.1 = (bf16[1,384,1536]{2,1,0:T(8,128)(2,1)S(1)}, bf16[1,384,1536]{2,1,0:T(8,128)(2,1)}, u32[]{:S(2)}) copy-start(bf16[1,384,1536]{2,1,0:T(8,128)(2,1)} %param.13) | copy-start | bytes 3538948
  0.6 12.2 %collective-permute-start.1 = (bf16[128,3072]{1,0:T(8,128)(2,1)}, bf16[128,3072]{1,0:T(8,128)(2,1)}, u32[]{:S(2)}, u32[]{:S(2)}) collective-permute-start(bf16[128,3072]{1,0:T(8,128)(2,1)} %lat.1), channel_id=1, source_target_pairs={{0,4},{1,3},{4,8},{5,1},{8,12},{9,5},{12,14},{13,9},{14,10},{15,13... | collective-permute-start | bytes 2359304 | tf_op jit(solution)/shard_map/ppermute | solution.py:621
  3.4 2.9 %collective-permute-start = (f32[3122]{0:T(1024)S(1)}, f32[3122]{0:T(1024)}, u32[]{:S(2)}, u32[]{:S(2)}) collective-permute-start(f32[3122]{0:T(1024)S(1)} %pad_maximum_fusion), channel_id=1, source_target_pairs={{0,1},{1,0},{2,3},{3,2},{4,5},{5,4},{6,7},{7,6},{8,9},{9,8},{10,11... | collective-permute-start | bytes 37472 | tf_op jit(solution)/shard_map/ppermute | solution.py:178
  4.5 50.2 %collective-permute-start.3 = (bf16[384,3072]{1,0:T(8,128)(2,1)}, bf16[384,3072]{1,0:T(8,128)(2,1)S(1)}, u32[]{:S(2)}, u32[]{:S(2)}) collective-permute-start(bf16[384,3072]{1,0:T(8,128)(2,1)} %bitcast.17), channel_id=1, source_target_pairs={{0,1},{1,0},{2,3},{3,2},{4,5},{5,4},{6,7},{7,6},{8,9},{9,8},{10,11... | collective-permute-start | bytes 7077896 | tf_op jit(solution)/shard_map/ppermute | solution.py:178
  12.8 11.5 %collective-permute-start.6 = (bf16[128,3072]{1,0:T(8,128)(2,1)}, bf16[128,3072]{1,0:T(8,128)(2,1)}, u32[]{:S(2)}, u32[]{:S(2)}) collective-permute-start(bf16[128,3072]{1,0:T(8,128)(2,1)} %collective-permute-done.1.refs_2_), channel_id=1, source_target_pairs={{0,4},{1,3},{4,8},{5,1},{8,12},{9,5},{12,14},{13,9},{14,10},{15,13... | collective-permute-start | bytes 2359304 | tf_op jit(solution)/shard_map/ppermute | solution.py:621
  17.0 11.4 %collective-permute-start.2 = (bf16[128,1536]{1,0:T(8,128)(2,1)}, bf16[128,1536]{1,0:T(8,128)(2,1)}, u32[]{:S(2)}, u32[]{:S(2)}) collective-permute-start(bf16[128,1536]{1,0:T(8,128)(2,1)} %get-tuple-element.51.refs_3_), channel_id=1, source_target_pairs={{0,4},{1,3},{4,8},{5,1},{8,12},{9,5},{12,14},{13,9},{14,10},{15,13... | collective-permute-start | bytes 1179656 | tf_op jit(solution)/shard_map/ppermute | solution.py:621
  18.3 36.2 %collective-permute-start.4 = (bf16[384,1536]{1,0:T(8,128)(2,1)}, bf16[384,1536]{1,0:T(8,128)(2,1)}, u32[]{:S(2)}, u32[]{:S(2)}) collective-permute-start(bf16[384,1536]{1,0:T(8,128)(2,1)} %bitcast.28), channel_id=1, source_target_pairs={{0,1},{1,0},{2,3},{3,2},{4,5},{5,4},{6,7},{7,6},{8,9},{9,8},{10,11... | collective-permute-start | bytes 3538952 | tf_op jit(solution)/shard_map/ppermute | solution.py:178
  20.5 34.0 %collective-permute-start.5 = (bf16[384,1536]{1,0:T(8,128)(2,1)S(1)}, bf16[384,1536]{1,0:T(8,128)(2,1)}, u32[]{:S(2)}, u32[]{:S(2)}) collective-permute-start(bf16[384,1536]{1,0:T(8,128)(2,1)S(1)} %bitcast.27), channel_id=1, source_target_pairs={{0,1},{1,0},{2,3},{3,2},{4,5},{5,4},{6,7},{7,6},{8,9},{9,8},{10,11... | collective-permute-start | bytes 3538952 | tf_op jit(solution)/shard_map/ppermute | solution.py:178
  24.3 18.8 %collective-permute-start.8 = (bf16[128,3072]{1,0:T(8,128)(2,1)}, bf16[128,3072]{1,0:T(8,128)(2,1)}, u32[]{:S(2)}, u32[]{:S(2)}) collective-permute-start(bf16[128,3072]{1,0:T(8,128)(2,1)} %collective-permute-done.6.refs_1_), channel_id=1, source_target_pairs={{0,4},{1,3},{4,8},{5,1},{8,12},{9,5},{12,14},{13,9},{14,10},{15,13... | collective-permute-start | bytes 2359304 | tf_op jit(solution)/shard_map/ppermute | solution.py:621
  28.5 12.6 %collective-permute-start.7 = (bf16[128,1536]{1,0:T(8,128)(2,1)}, bf16[128,1536]{1,0:T(8,128)(2,1)}, u32[]{:S(2)}, u32[]{:S(2)}) collective-permute-start(bf16[128,1536]{1,0:T(8,128)(2,1)} %collective-permute-done.2.refs_4_), channel_id=1, source_target_pairs={{0,4},{1,3},{4,8},{5,1},{8,12},{9,5},{12,14},{13,9},{14,10},{15,13... | collective-permute-start | bytes 1179656 | tf_op jit(solution)/shard_map/ppermute | solution.py:621
  31.2 11.3 %copy-start.22 = (s32[10]{0:T(128)}, s32[10]{0:T(128)S(1)}, u32[]{:S(2)}) copy-start(s32[10]{0:T(128)S(1)} %select_reduce_fusion) | copy-start | bytes 124
  41.1 7.2 %collective-permute-start.9 = (bf16[128,1536]{1,0:T(8,128)(2,1)}, bf16[128,1536]{1,0:T(8,128)(2,1)}, u32[]{:S(2)}, u32[]{:S(2)}) collective-permute-start(bf16[128,1536]{1,0:T(8,128)(2,1)} %collective-permute-done.7.refs_2_), channel_id=1, source_target_pairs={{0,4},{1,3},{4,8},{5,1},{8,12},{9,5},{12,14},{13,9},{14,10},{15,13... | collective-permute-start | bytes 1179656 | tf_op jit(solution)/shard_map/ppermute | solution.py:621
  44.1 10.6 %collective-permute-start.10 = (bf16[64,3072]{1,0:T(8,128)(2,1)S(1)}, bf16[64,3072]{1,0:T(8,128)(2,1)}, u32[]{:S(2)}, u32[]{:S(2)}) collective-permute-start(bf16[64,3072]{1,0:T(8,128)(2,1)S(1)} %constant_dynamic-slice_fusion.3), channel_id=1, source_target_pairs={{0,4},{1,3},{4,8},{5,1},{8,12},{9,5},{12,14},{13,9},{14,10},{15,13... | collective-permute-start | bytes 1179656 | tf_op jit(solution)/shard_map/ppermute | solution.py:621
  49.3 5.4 %collective-permute-start.11 = (bf16[64,1536]{1,0:T(8,128)(2,1)S(1)}, bf16[64,1536]{1,0:T(8,128)(2,1)S(1)}, u32[]{:S(2)}, u32[]{:S(2)}) collective-permute-start(bf16[64,1536]{1,0:T(8,128)(2,1)S(1)} %constant_dynamic-slice_fusion.2), channel_id=1, source_target_pairs={{0,4},{1,3},{4,8},{5,1},{8,12},{9,5},{12,14},{13,9},{14,10},{15,13... | collective-permute-start | bytes 589832 | tf_op jit(solution)/shard_map/ppermute | solution.py:621
  65.6 14.8 %collective-permute-start.21 = (bf16[64,1664]{1,0:T(8,128)(2,1)}, bf16[64,1664]{1,0:T(8,128)(2,1)S(1)}, u32[]{:S(2)}, u32[]{:S(2)}) collective-permute-start(bf16[64,1664]{1,0:T(8,128)(2,1)} %shard_map.131), channel_id=1, source_target_pairs={{0,2},{1,5},{4,0},{5,9},{8,4},{9,13},{12,8},{13,15},{14,12},{15,11... | collective-permute-start | bytes 638984 | tf_op jit(solution)/shard_map/ppermute | solution.py:622
  70.0 15.0 %collective-permute-start.16 = (bf16[64,1536]{1,0:T(8,128)(2,1)}, bf16[64,1536]{1,0:T(8,128)(2,1)S(1)}, u32[]{:S(2)}, u32[]{:S(2)}) collective-permute-start(bf16[64,1536]{1,0:T(8,128)(2,1)} %shard_map.126), channel_id=1, source_target_pairs={{0,2},{1,5},{4,0},{5,9},{8,4},{9,13},{12,8},{13,15},{14,12},{15,11... | collective-permute-start | bytes 589832 | tf_op jit(solution)/shard_map/ppermute | solution.py:622
  83.8 15.6 %collective-permute-start.22 = (bf16[128,1664]{1,0:T(8,128)(2,1)}, bf16[128,1664]{1,0:T(8,128)(2,1)S(1)}, u32[]{:S(2)}, u32[]{:S(2)}) collective-permute-start(bf16[128,1664]{1,0:T(8,128)(2,1)} %shard_map.132), channel_id=1, source_target_pairs={{0,2},{1,5},{4,0},{5,9},{8,4},{9,13},{12,8},{13,15},{14,12},{15,11... | collective-permute-start | bytes 1277960 | tf_op jit(solution)/shard_map/ppermute | solution.py:622
  87.9 15.2 %collective-permute-start.17 = (bf16[128,1536]{1,0:T(8,128)(2,1)}, bf16[128,1536]{1,0:T(8,128)(2,1)S(1)}, u32[]{:S(2)}, u32[]{:S(2)}) collective-permute-start(bf16[128,1536]{1,0:T(8,128)(2,1)} %shard_map.127), channel_id=1, source_target_pairs={{0,2},{1,5},{4,0},{5,9},{8,4},{9,13},{12,8},{13,15},{14,12},{15,11... | collective-permute-start | bytes 1179656 | tf_op jit(solution)/shard_map/ppermute | solution.py:622
  103.0 13.9 %collective-permute-start.23 = (bf16[128,1664]{1,0:T(8,128)(2,1)}, bf16[128,1664]{1,0:T(8,128)(2,1)S(1)}, u32[]{:S(2)}, u32[]{:S(2)}) collective-permute-start(bf16[128,1664]{1,0:T(8,128)(2,1)} %shard_map.133), channel_id=1, source_target_pairs={{0,2},{1,5},{4,0},{5,9},{8,4},{9,13},{12,8},{13,15},{14,12},{15,11... | collective-permute-start | bytes 1277960 | tf_op jit(solution)/shard_map/ppermute | solution.py:622
  106.0 14.7 %collective-permute-start.18 = (bf16[128,1536]{1,0:T(8,128)(2,1)}, bf16[128,1536]{1,0:T(8,128)(2,1)S(1)}, u32[]{:S(2)}, u32[]{:S(2)}) collective-permute-start(bf16[128,1536]{1,0:T(8,128)(2,1)} %shard_map.128), channel_id=1, source_target_pairs={{0,2},{1,5},{4,0},{5,9},{8,4},{9,13},{12,8},{13,15},{14,12},{15,11... | collective-permute-start | bytes 1179656 | tf_op jit(solution)/shard_map/ppermute | solution.py:622
  120.5 7.2 %collective-permute-start.24 = (bf16[128,1664]{1,0:T(8,128)(2,1)}, bf16[128,1664]{1,0:T(8,128)(2,1)S(1)}, u32[]{:S(2)}, u32[]{:S(2)}) collective-permute-start(bf16[128,1664]{1,0:T(8,128)(2,1)} %shard_map.134), channel_id=1, source_target_pairs={{0,2},{1,5},{4,0},{5,9},{8,4},{9,13},{12,8},{13,15},{14,12},{15,11... | collective-permute-start | bytes 1277960 | tf_op jit(solution)/shard_map/ppermute | solution.py:622
  123.7 14.1 %collective-permute-start.19 = (bf16[128,1536]{1,0:T(8,128)(2,1)}, bf16[128,1536]{1,0:T(8,128)(2,1)S(1)}, u32[]{:S(2)}, u32[]{:S(2)}) collective-permute-start(bf16[128,1536]{1,0:T(8,128)(2,1)} %shard_map.129), channel_id=1, source_target_pairs={{0,2},{1,5},{4,0},{5,9},{8,4},{9,13},{12,8},{13,15},{14,12},{15,11... | collective-permute-start | bytes 1179656 | tf_op jit(solution)/shard_map/ppermute | solution.py:622
  131.3 11.8 %collective-permute-start.25 = (bf16[128,1664]{1,0:T(8,128)(2,1)}, bf16[128,1664]{1,0:T(8,128)(2,1)S(1)}, u32[]{:S(2)}, u32[]{:S(2)}) collective-permute-start(bf16[128,1664]{1,0:T(8,128)(2,1)} %shard_map.135.head_a), channel_id=1, source_target_pairs={{0,1},{1,0},{2,3},{3,2},{4,5},{5,4},{6,7},{7,6},{8,9},{9,8},{10,11... | collective-permute-start | bytes 1277960 | tf_op jit(solution)/shard_map/ppermute | solution.py:178
  140.9 2.2 %collective-permute-start.20 = (bf16[128,1536]{1,0:T(8,128)(2,1)}, bf16[128,1536]{1,0:T(8,128)(2,1)S(1)}, u32[]{:S(2)}, u32[]{:S(2)}) collective-permute-start(bf16[128,1536]{1,0:T(8,128)(2,1)} %shard_map.130.update_a), channel_id=1, source_target_pairs={{0,1},{1,0},{2,3},{3,2},{4,5},{5,4},{6,7},{7,6},{8,9},{9,8},{10,11... | collective-permute-start | bytes 1179656 | tf_op jit(solution)/shard_map/ppermute | solution.py:178
  148.7 24.0 %copy-start.28 = (bf16[64,3456]{1,0:T(8,128)(2,1)S(1)}, bf16[64,3456]{1,0:T(8,128)(2,1)}, u32[]{:S(2)}) copy-start(bf16[64,3456]{1,0:T(8,128)(2,1)} %get-tuple-element.33) | copy-start | bytes 1327108
  148.7 7.1 %collective-permute-start.30 = (bf16[128,1536]{1,0:T(8,128)(2,1)}, bf16[128,1536]{1,0:T(8,128)(2,1)S(1)}, u32[]{:S(2)}, u32[]{:S(2)}) collective-permute-start(bf16[128,1536]{1,0:T(8,128)(2,1)} %get-tuple-element.47.refs_11_), channel_id=1, source_target_pairs={{0,4},{1,3},{4,8},{5,1},{8,12},{9,5},{12,14},{13,9},{14,10},{15,13... | collective-permute-start | bytes 1179656 | tf_op jit(solution)/shard_map/ppermute | solution.py:621
  148.9 11.2 %collective-permute-start.26 = (bf16[128,1536]{1,0:T(8,128)(2,1)}, bf16[128,1536]{1,0:T(8,128)(2,1)S(1)}, u32[]{:S(2)}, u32[]{:S(2)}) collective-permute-start(bf16[128,1536]{1,0:T(8,128)(2,1)} %get-tuple-element.46.refs_10_), channel_id=1, source_target_pairs={{0,4},{1,3},{4,8},{5,1},{8,12},{9,5},{12,14},{13,9},{14,10},{15,13... | collective-permute-start | bytes 1179656 | tf_op jit(solution)/shard_map/ppermute | solution.py:621
  149.0 29.1 %collective-permute-start.14 = (bf16[128,3456]{1,0:T(8,128)(2,1)S(1)}, bf16[128,3456]{1,0:T(8,128)(2,1)S(1)}, u32[]{:S(2)}, u32[]{:S(2)}) collective-permute-start(bf16[128,3456]{1,0:T(8,128)(2,1)S(1)} %copy-done.25), channel_id=1, source_target_pairs={{0,1},{1,0},{2,3},{3,2},{4,5},{5,4},{6,7},{7,6},{8,9},{9,8},{10,11... | collective-permute-start | bytes 2654216 | tf_op jit(solution)/shard_map/ppermute | solution.py:178
  152.1 34.2 %collective-permute-start.12 = (bf16[192,3456]{1,0:T(8,128)(2,1)}, bf16[192,3456]{1,0:T(8,128)(2,1)S(1)}, u32[]{:S(2)}, u32[]{:S(2)}) collective-permute-start(bf16[192,3456]{1,0:T(8,128)(2,1)} %get-tuple-element.30), channel_id=1, source_target_pairs={{0,1},{1,0},{2,3},{3,2},{4,5},{5,4},{6,7},{7,6},{8,9},{9,8},{10,11... | collective-permute-start | bytes 3981320 | tf_op jit(solution)/shard_map/ppermute | solution.py:178
  152.2 34.1 %collective-permute-start.13 = (bf16[128,3456]{1,0:T(8,128)(2,1)}, bf16[128,3456]{1,0:T(8,128)(2,1)S(1)}, u32[]{:S(2)}, u32[]{:S(2)}) collective-permute-start(bf16[128,3456]{1,0:T(8,128)(2,1)} %get-tuple-element.31), channel_id=1, source_target_pairs={{0,1},{1,0},{2,3},{3,2},{4,5},{5,4},{6,7},{7,6},{8,9},{9,8},{10,11... | collective-permute-start | bytes 2654216 | tf_op jit(solution)/shard_map/ppermute | solution.py:178
  155.8 18.1 %copy-start.8 = (bf16[128,1536]{1,0:T(8,128)(2,1)}, bf16[128,1536]{1,0:T(8,128)(2,1)S(1)}, u32[]{:S(2)}) copy-start(bf16[128,1536]{1,0:T(8,128)(2,1)S(1)} %collective-permute-done.30.refs_16_) | copy-start | bytes 1179652
  155.8 8.4 %collective-permute-start.31 = (bf16[128,1536]{1,0:T(8,128)(2,1)S(1)}, bf16[128,1536]{1,0:T(8,128)(2,1)S(1)}, u32[]{:S(2)}, u32[]{:S(2)}) collective-permute-start(bf16[128,1536]{1,0:T(8,128)(2,1)S(1)} %collective-permute-done.30.refs_16_), channel_id=1, source_target_pairs={{0,4},{1,3},{4,8},{5,1},{8,12},{9,5},{12,14},{13,9},{14,10},{15,13... | collective-permute-start | bytes 1179656 | tf_op jit(solution)/shard_map/ppermute | solution.py:621
  160.0 13.9 %copy-start.9 = (bf16[128,1536]{1,0:T(8,128)(2,1)}, bf16[128,1536]{1,0:T(8,128)(2,1)S(1)}, u32[]{:S(2)}) copy-start(bf16[128,1536]{1,0:T(8,128)(2,1)S(1)} %collective-permute-done.26.refs_12_) | copy-start | bytes 1179652
  160.0 8.4 %collective-permute-start.27 = (bf16[128,1536]{1,0:T(8,128)(2,1)S(1)}, bf16[128,1536]{1,0:T(8,128)(2,1)S(1)}, u32[]{:S(2)}, u32[]{:S(2)}) collective-permute-start(bf16[128,1536]{1,0:T(8,128)(2,1)S(1)} %collective-permute-done.26.refs_12_), channel_id=1, source_target_pairs={{0,4},{1,3},{4,8},{5,1},{8,12},{9,5},{12,14},{13,9},{14,10},{15,13... | collective-permute-start | bytes 1179656 | tf_op jit(solution)/shard_map/ppermute | solution.py:621
  164.3 13.8 %copy-start.10 = (bf16[128,1536]{1,0:T(8,128)(2,1)}, bf16[128,1536]{1,0:T(8,128)(2,1)S(1)}, u32[]{:S(2)}) copy-start(bf16[128,1536]{1,0:T(8,128)(2,1)S(1)} %collective-permute-done.31.refs_17_) | copy-start | bytes 1179652
  164.3 8.4 %collective-permute-start.32 = (bf16[128,1536]{1,0:T(8,128)(2,1)S(1)}, bf16[128,1536]{1,0:T(8,128)(2,1)S(1)}, u32[]{:S(2)}, u32[]{:S(2)}) collective-permute-start(bf16[128,1536]{1,0:T(8,128)(2,1)S(1)} %collective-permute-done.31.refs_17_), channel_id=1, source_target_pairs={{0,4},{1,3},{4,8},{5,1},{8,12},{9,5},{12,14},{13,9},{14,10},{15,13... | collective-permute-start | bytes 1179656 | tf_op jit(solution)/shard_map/ppermute | solution.py:621
  168.5 9.6 %copy-start.11 = (bf16[128,1536]{1,0:T(8,128)(2,1)}, bf16[128,1536]{1,0:T(8,128)(2,1)S(1)}, u32[]{:S(2)}) copy-start(bf16[128,1536]{1,0:T(8,128)(2,1)S(1)} %collective-permute-done.27.refs_13_) | copy-start | bytes 1179652
  168.5 8.4 %collective-permute-start.28 = (bf16[128,1536]{1,0:T(8,128)(2,1)S(1)}, bf16[128,1536]{1,0:T(8,128)(2,1)S(1)}, u32[]{:S(2)}, u32[]{:S(2)}) collective-permute-start(bf16[128,1536]{1,0:T(8,128)(2,1)S(1)} %collective-permute-done.27.refs_13_), channel_id=1, source_target_pairs={{0,4},{1,3},{4,8},{5,1},{8,12},{9,5},{12,14},{13,9},{14,10},{15,13... | collective-permute-start | bytes 1179656 | tf_op jit(solution)/shard_map/ppermute | solution.py:621
  172.7 15.2 %copy-start.2 = (bf16[128,1536]{1,0:T(8,128)(2,1)}, bf16[128,1536]{1,0:T(8,128)(2,1)S(1)}, u32[]{:S(2)}) copy-start(bf16[128,1536]{1,0:T(8,128)(2,1)S(1)} %collective-permute-done.32.refs_18_) | copy-start | bytes 1179652
  172.7 4.4 %collective-permute-start.15 = (bf16[64,3456]{1,0:T(8,128)(2,1)S(1)}, bf16[64,3456]{1,0:T(8,128)(2,1)S(1)}, u32[]{:S(2)}, u32[]{:S(2)}) collective-permute-start(bf16[64,3456]{1,0:T(8,128)(2,1)S(1)} %copy-done.28), channel_id=1, source_target_pairs={{0,1},{1,0},{2,3},{3,2},{4,5},{5,4},{6,7},{7,6},{8,9},{9,8},{10,11... | collective-permute-start | bytes 1327112 | tf_op jit(solution)/shard_map/ppermute | solution.py:178
  176.9 11.0 %copy-start.3 = (bf16[128,1536]{1,0:T(8,128)(2,1)}, bf16[128,1536]{1,0:T(8,128)(2,1)S(1)}, u32[]{:S(2)}) copy-start(bf16[128,1536]{1,0:T(8,128)(2,1)S(1)} %collective-permute-done.28.refs_14_) | copy-start | bytes 1179652
  176.9 5.3 %collective-permute-start.33 = (bf16[64,1536]{1,0:T(8,128)(2,1)S(1)}, bf16[64,1536]{1,0:T(8,128)(2,1)S(1)}, u32[]{:S(2)}, u32[]{:S(2)}) collective-permute-start(bf16[64,1536]{1,0:T(8,128)(2,1)S(1)} %constant_dynamic-slice_fusion), channel_id=1, source_target_pairs={{0,4},{1,3},{4,8},{5,1},{8,12},{9,5},{12,14},{13,9},{14,10},{15,13... | collective-permute-start | bytes 589832 | tf_op jit(solution)/shard_map/ppermute | solution.py:621
  177.9 5.9 %collective-permute-start.29 = (bf16[64,1536]{1,0:T(8,128)(2,1)S(1)}, bf16[64,1536]{1,0:T(8,128)(2,1)S(1)}, u32[]{:S(2)}, u32[]{:S(2)}) collective-permute-start(bf16[64,1536]{1,0:T(8,128)(2,1)S(1)} %constant_dynamic-slice_fusion.1), channel_id=1, source_target_pairs={{0,4},{1,3},{4,8},{5,1},{8,12},{9,5},{12,14},{13,9},{14,10},{15,13... | collective-permute-start | bytes 589832 | tf_op jit(solution)/shard_map/ppermute | solution.py:621
  178.1 9.7 %copy-start.26 = (bf16[128,3456]{1,0:T(8,128)(2,1)}, bf16[128,3456]{1,0:T(8,128)(2,1)S(1)}, u32[]{:S(2)}) copy-start(bf16[128,3456]{1,0:T(8,128)(2,1)S(1)} %collective-permute-done.14.refs_8_) | copy-start | bytes 2654212
  178.1 8.2 %collective-permute-start.34 = (bf16[128,1536]{1,0:T(8,128)(2,1)S(1)}, bf16[128,1536]{1,0:T(8,128)(2,1)S(1)}, u32[]{:S(2)}, u32[]{:S(2)}) collective-permute-start(bf16[128,1536]{1,0:T(8,128)(2,1)S(1)} %broadcast_select_fusion.2), channel_id=1, source_target_pairs={{0,1},{1,0},{2,3},{3,2},{4,5},{5,4},{6,7},{7,6},{8,9},{9,8},{10,11... | collective-permute-start | bytes 1179656 | tf_op jit(solution)/shard_map/ppermute | solution.py:178
  182.2 4.2 %collective-permute-start.35 = (bf16[128,1536]{1,0:T(8,128)(2,1)S(1)}, bf16[128,1536]{1,0:T(8,128)(2,1)S(1)}, u32[]{:S(2)}, u32[]{:S(2)}) collective-permute-start(bf16[128,1536]{1,0:T(8,128)(2,1)S(1)} %broadcast_select_fusion.1), channel_id=1, source_target_pairs={{0,1},{1,0},{2,3},{3,2},{4,5},{5,4},{6,7},{7,6},{8,9},{9,8},{10,11... | collective-permute-start | bytes 1179656 | tf_op jit(solution)/shard_map/ppermute | solution.py:178
  183.8 4.0 %collective-permute-start.36 = (bf16[128,1536]{1,0:T(8,128)(2,1)S(1)}, bf16[128,1536]{1,0:T(8,128)(2,1)S(1)}, u32[]{:S(2)}, u32[]{:S(2)}) collective-permute-start(bf16[128,1536]{1,0:T(8,128)(2,1)S(1)} %broadcast_select_fusion), channel_id=1, source_target_pairs={{0,1},{1,0},{2,3},{3,2},{4,5},{5,4},{6,7},{7,6},{8,9},{9,8},{10,11... | collective-permute-start | bytes 1179656 | tf_op jit(solution)/shard_map/ppermute | solution.py:178
  186.2 1.6 collective-permute-start.37
  (24 other events, 39.5 us)
